TPU v7x, 512 devices: a whole 4x4x16 slice. The times are simulated.
512 devices in a mesh: dp: 2 (over core), ctx: 32 (over x, z_lo), tensor: 8 (over z_hi, y).
Axes of the slice: x: 4, y: 4, z: 16 (z_hi: 2, z_lo: 8; z = z_hi * 8 + z_lo), core: 2. Of those that a mesh axis runs over, the one named last changes fastest.
Arguments:
- tokens: bfloat16 [2, 4096, 2048], P('dp', 'ctx', 'tensor'), may hold values from -6 to 6
- cotangent: bfloat16 [2, 4096, 2048], P('dp', 'ctx', 'tensor'), may hold values from -6 to 6
- w_value: bfloat16 [2048, 2048], P('ctx', 'tensor'), may hold values from -0.125 to 0.125
- w_gate: bfloat16 [2048, 2048], P('ctx', 'tensor'), may hold values from -0.125 to 0.125
- decay_rate: float32 [4, 2048], P(None, 'tensor'), as said below
- residue: float32 [4, 2048], P(None, 'tensor'), may hold values from -4 to 4
- skip_gain: float32 [2048], P('tensor'), may hold values from -4 to 4
- contig_len: int32 [2, 8], P('dp'), may hold values from 1 to 1536, 4096 in all within a row
Outputs:
- output: bfloat16 [2, 4096, 2048], P('dp', 'ctx', 'tensor')
- grad_tokens: bfloat16 [2, 4096, 2048], P('dp', 'ctx', 'tensor')
- grad_w_value: float32 [2048, 2048], P('ctx', 'tensor')
- grad_w_gate: float32 [2048, 2048], P('ctx', 'tensor')
- grad_skip: float32 [2048], P('tensor')
- grad_residue: float32 [4, 2048], P(None, 'tensor')
- grad_rate: float32 [4, 2048], P(None, 'tensor')
Inputs may be any that keep to these rules, and one draw needn't show every extreme that they name: `contig_len`: each row's lengths sum to 4096; the largest of each row is exactly 1536. `decay_rate`: every rate lies between 0.25 / 4096 and 1 / 30.
All inputs are finite; a program needn't handle non-finite values.
Results may differ from a plain program's by a relative error of at most 0.012.
Values may be sent and summed in bfloat16 or wider, within the bound.
A program may use at most 64 MiB of HBM per device.

v0:
```python
import jax
import jax.numpy as jnp
from jax import lax
from jax.sharding import PartitionSpec as P


def carried_in(part, axis, combine, identity, reverse):
    count = lax.axis_size(axis)
    place = lax.axis_index(axis)
    ahead = count - 1 - place if reverse else place
    gathered = jax.tree.map(lambda a: lax.all_gather(a, axis), part)
    state = jax.tree.map(lambda a, e: jnp.zeros_like(a) + jnp.asarray(e, a.dtype), part, identity)

    def one(hop, state):
        source = count - 1 - hop if reverse else hop
        return combine(
            state, jax.tree.map(lambda a: lax.dynamic_index_in_dim(a, source, 0, False), gathered)
        )

    return lax.fori_loop(0, ahead, one, state)


def link(first, second):
    return (first[0] * second[0], second[0] * first[1] + second[1])


def body(tokens, cotangent, w_value, w_gate, decay_rate, residue, skip_gain, contig_len):
    rows, span, width = tokens.shape
    flat = tokens.reshape(rows * span, width)
    feats = lax.all_gather(flat, "tensor", axis=1, tiled=True)
    paired_w = jnp.concatenate([w_value, w_gate], axis=1)
    whole = lax.all_gather(paired_w, "ctx", axis=0, tiled=True)
    both = jnp.dot(feats, whole, preferred_element_type=jnp.float32)
    value = both[:, :width].reshape(rows, span, width)
    gate = both[:, width:].reshape(rows, span, width)
    me = lax.axis_index("ctx")
    first = me * span
    positions = first + jnp.arange(span, dtype=jnp.int32)
    starts = jnp.cumsum(contig_len, axis=1) - contig_len
    here = starts[:, None, :]
    place = positions[None, :, None]
    reset = jnp.any(place == here, axis=2).astype(jnp.float32)
    reset_next = jnp.any(place + 1 == here, axis=2).astype(jnp.float32)
    clear_fwd = jnp.all((here < first) | (here > place), axis=2).astype(jnp.float32)
    clear_back = jnp.all((here <= place) | (here > first + span), axis=2).astype(jnp.float32)
    pole = jnp.exp(-decay_rate)
    factor = jnp.sqrt(-jnp.expm1(-2.0 * decay_rate))
    weight_mode = residue * factor
    steps_in = (jnp.arange(span, dtype=jnp.int32) + 1).astype(jnp.float32)
    decay_fwd = jnp.exp(-decay_rate[None] * steps_in[:, None, None])
    decay_back = decay_fwd[::-1]
    keep = (1.0 - reset)[:, :, None, None] * pole
    drive = jnp.broadcast_to(value[:, :, None, :], keep.shape)
    local = lax.associative_scan(link, (keep, drive), axis=1)[1]
    scale_end = decay_fwd[-1][None] * clear_fwd[:, -1][:, None, None]
    end_state = local[:, -1]
    _, incoming = carried_in(
        (scale_end, end_state),
        "ctx",
        link,
        (jnp.ones_like(scale_end), jnp.zeros_like(end_state)),
        False,
    )
    state = local + decay_fwd[None] * clear_fwd[:, :, None, None] * incoming[:, None]
    mixed = jnp.sum(weight_mode * state, axis=2) + skip_gain * value
    output = (gate * mixed).astype(jnp.bfloat16)
    upstream = cotangent.astype(jnp.float32)
    grad_mixed = upstream * gate
    grad_gate = upstream * mixed
    keep_back = (1.0 - reset_next)[:, :, None, None] * pole
    source = grad_mixed[:, :, None, :] * weight_mode
    local_back = lax.associative_scan(link, (keep_back[:, ::-1], source[:, ::-1]), axis=1)[1][
        :, ::-1
    ]
    scale_top = decay_back[0][None] * clear_back[:, 0][:, None, None]
    top_state = local_back[:, 0]
    _, incoming_back = carried_in(
        (scale_top, top_state),
        "ctx",
        link,
        (jnp.ones_like(scale_top), jnp.zeros_like(top_state)),
        True,
    )
    grad_state = (
        local_back + decay_back[None] * clear_back[:, :, None, None] * incoming_back[:, None]
    )
    grad_value = jnp.sum(grad_state, axis=2) + skip_gain * grad_mixed
    skip_part = jnp.sum(grad_mixed * value, axis=(0, 1))
    paired_part = jnp.sum(grad_mixed[:, :, None, :] * state, axis=(0, 1))
    carried_part = jnp.sum(grad_state * (state - drive), axis=(0, 1))
    grad_skip, paired, carried = lax.psum((skip_part, paired_part, carried_part), ("dp", "ctx"))
    grad_residue = factor * paired
    grad_rate = -carried + residue * jnp.exp(-2.0 * decay_rate) / factor * paired
    cot_both = (
        jnp.concatenate([grad_value, grad_gate], axis=2)
        .astype(jnp.bfloat16)
        .reshape(rows * span, 2 * width)
    )
    contract = (((1,), (1,)), ((), ()))
    term = lax.dot_general(cot_both, whole, contract, preferred_element_type=jnp.float32)
    grad_tokens = lax.psum_scatter(
        term.astype(jnp.bfloat16), "tensor", scatter_dimension=1, tiled=True
    )
    grad_tokens = grad_tokens.reshape(rows, span, width)
    slabs = lax.all_to_all(feats, "ctx", split_axis=1, concat_axis=0, tiled=True)
    grad_w = lax.dot_general(
        slabs,
        lax.all_gather(cot_both, "ctx", axis=0, tiled=True),
        (((0,), (0,)), ((), ())),
        preferred_element_type=jnp.float32,
    )
    grad_w = lax.psum(grad_w, "dp")
    return (
        output,
        grad_tokens,
        grad_w[:, :width],
        grad_w[:, width:],
        grad_skip,
        grad_residue,
        grad_rate,
    )


def solution(mesh):
    in_specs = (
        P("dp", "ctx", "tensor"),
        P("dp", "ctx", "tensor"),
        P("ctx", "tensor"),
        P("ctx", "tensor"),
        P(None, "tensor"),
        P(None, "tensor"),
        P("tensor"),
        P("dp", None),
    )
    out_specs = (
        P("dp", "ctx", "tensor"),
        P("dp", "ctx", "tensor"),
        P("ctx", "tensor"),
        P("ctx", "tensor"),
        P("tensor"),
        P(None, "tensor"),
        P(None, "tensor"),
    )
    return jax.shard_map(body, mesh=mesh, in_specs=in_specs, out_specs=out_specs, check_vma=False)
```

profile of v0, /device:TPU:1, one launch (start us, length us, event | category | flops | bytes accessed | tf_op | source)
XLA Modules:
  0.0 1118.4 jit_solution(10773666285794444207)
XLA Ops:
  7.2 1.4 pad_maximum_fusion.5
  8.7 0.8 reduce_window_sum.11
  12.6 1.0 copy.23
  13.6 0.7 fusion.29
  14.7 0.7 slice.435
  16.0 118.4 %all-gather.2 = f32[32,4,256]{2,1,0:T(4,128)} all-gather(f32[1,4,256]{2,1,0:T(4,128)S(1)} %get-tuple-element.204), channel_id=4, replica_groups=mesh['dp'=2,'ctx'=32,'tensor'=8] {'ctx'}, dimensions={0}, use_global_device_ids=true | all-gather | bytes 135168 | tf_op jit(solution)/shard_map/all_gather | solution.py:11
  134.4 104.2 %all-gather.1 = f32[32,4,256]{2,1,0:T(4,128)} all-gather(f32[1,4,256]{2,1,0:T(4,128)S(1)} %get-tuple-element.205), channel_id=3, replica_groups=mesh['dp'=2,'ctx'=32,'tensor'=8] {'ctx'}, dimensions={0}, use_global_device_ids=true | all-gather | bytes 135168 | tf_op jit(solution)/shard_map/all_gather | solution.py:11
  238.6 59.5 %all-gather = bf16[1,128,2048]{1,2,0:T(8,128)(2,1)S(1)} all-gather(bf16[1,128,256]{1,2,0:T(8,128)(2,1)S(1)} %copy.23), channel_id=2, replica_groups=mesh['dp'=2,'ctx'=32,'tensor'=8] {'tensor'}, dimensions={2}, use_global_device_ids=true | all-gather | bytes 589824 | tf_op jit(solution)/shard_map/all_gather | solution.py:30
  298.2 2.1 convolution_bitcast_fusion
  302.9 0.8 slice.489
  305.3 0.7 pad_maximum_fusion.7
  307.8 0.8 pad.112
  308.7 0.8 pad.113
  310.3 1.0 slice_multiply_fusion
  313.4 0.7 pad_maximum_fusion.10
  314.2 0.7 pad_maximum_fusion.8
  315.2 0.7 pad_maximum_fusion.6
  316.3 0.7 fusion.9
  317.1 99.2 %all_gather.34 = f32[32,1,4,256]{3,2,1,0:T(4,128)S(1)} all-gather(f32[1,1,4,256]{3,2,1,0:T(4,128)} %slice_add_fusion.10), channel_id=1, replica_groups=mesh['dp'=2,'ctx'=32,'tensor'=8] {'ctx'}, dimensions={0}, use_global_device_ids=true | all-gather | bytes 135168 | tf_op jit(solution)/shard_map/all_gather | solution.py:11
  416.3 21.3 %while.27 = (s32[]{:T(128)}, f32[1,4,256]{2,1,0:T(4,128)S(1)}, s32[]{:T(128)}, f32[32,1,4,256]{3,2,1,0:T(4,128)}, f32[32,1,4,256]{3,2,1,0:T(4,128)S(1)}, /*index=5*/s32[]{:T(128)}, s32[]{:T(128)}, s32[]{:T(128)}, s32[]{:T(128)}) while((s32[]{:T(128)}, f32[1,4,256]{2,1,0:T(4,128)S(1)}, s32[]{:T(128)}, f32[32,1,4,256]{3,2,1,0:T(4,128)}, ...), condition=%wide.region_9.10_spmd, body=%wide.region_8.9_spmd.sunk | while | flops 2054 | bytes 16535 | solution.py:20
  418.3 0.7 bitcast_add_fusion.7
  419.0 0.7 bitcast_add_fusion.7
  420.4 0.7 bitcast_add_fusion.7
  423.2 0.7 bitcast_add_fusion.7
  423.8 0.7 bitcast_add_fusion.7
  425.2 0.7 bitcast_add_fusion.7
  426.6 0.7 bitcast_add_fusion.7
  427.3 0.7 bitcast_add_fusion.7
  428.7 0.7 bitcast_add_fusion.7
  429.4 0.7 bitcast_add_fusion.7
  430.7 0.7 bitcast_add_fusion.7
  432.1 0.7 bitcast_add_fusion.7
  432.8 0.7 bitcast_add_fusion.7
  434.2 0.7 bitcast_add_fusion.7
  436.2 0.7 bitcast_add_fusion.7
  437.6 0.9 pad_maximum_fusion.2
  439.4 0.8 add.297
  440.2 1.0 fusion.4
  441.9 0.8 pad.98
  442.7 22.1 %pad.99 = f32[1,128,4,256]{3,2,1,0:T(4,128)S(1)} pad(f32[1,64,4,256]{3,2,1,0:T(4,128)} %add.297, f32[]{:T(128)} %constant.69.clone.1), padding=0_0_0x1_0_1x0_0_0x0_0_0 | pad | bytes 786436 | tf_op jit(solution)/shard_map/pad | solution.py:54
  464.8 98.4 %all_gather.31 = f32[32,1,4,256]{3,2,1,0:T(4,128)S(1)} all-gather(f32[1,1,4,256]{3,2,1,0:T(4,128)S(1)} %slice_add_fusion.12), channel_id=1, replica_groups=mesh['dp'=2,'ctx'=32,'tensor'=8] {'ctx'}, dimensions={0}, use_global_device_ids=true | all-gather | bytes 135168 | tf_op jit(solution)/shard_map/all_gather | solution.py:11
  563.2 2.3 multiply_reduce_fusion
  566.4 44.6 %all_to_all.19 = bf16[128,32,64]{0,2,1:T(8,128)(2,1)S(1)} all-to-all(bf16[128,32,64]{0,2,1:T(8,128)(2,1)S(1)} %bitcast.93), channel_id=1, replica_groups=mesh['dp'=2,'ctx'=32,'tensor'=8] {'ctx'}, dimensions={1} | all-to-all | bytes 1048576 | tf_op jit(solution)/shard_map/all_to_all | solution.py:105
  611.0 244.9 %all-gather.8.cloned.1.call-done = bf16[4096,512]{1,0:T(8,128)(2,1)} async-done(((bf16[128,512]{1,0:T(8,128)(2,1)}), bf16[4096,512]{1,0:T(8,128)(2,1)}) %all-gather.8.cloned.1.call-update) | async-done | bytes 4194320 | tf_op jit(solution)/shard_map/all_gather | solution.py:108
  855.9 3.7 convolution_bitcast_fusion.1
  859.6 1.6 convolution_convert_fusion
  861.3 247.7 %all-reduce.28 = (f32[256]{0:T(256)}, f32[4,256]{1,0:T(4,128)S(1)}, f32[4,256]{1,0:T(4,128)S(1)}) all-reduce(f32[256]{0:T(256)S(1)} %get-tuple-element.210, f32[4,256]{1,0:T(4,128)S(1)} %get-tuple-element.169, f32[4,256]{1,0:T(4,128)S(1)} %get-tuple-element.167), channel_id=1, replica_groups=mesh['dp'=2,'ctx'=32,'tensor'=8] {'dp','ctx'}, use_global_device_ids=true, to_apply=%region_14.15 | all-reduce | flops 2304 | bytes 18432 | tf_op jit(solution)/shard_map/psum | solution.py:91
  1110.3 1.5 fusion.33
  (155 shorter events, 27.6 us)
Async XLA Ops:
  7.2 291.0 %all-gather.6.cloned.1.call-start = ((), (), s32[]{:S(2)}) async-start(), calls=%async_computation.2 | async-start | bytes 2162688 | tf_op jit(solution)/shard_map/all_gather | solution.py:32
  8.6 847.2 %all-gather.8.cloned.1.call-start = ((), (), s32[]{:S(2)}) async-start(), calls=%async_computation.4 | async-start | bytes 4325376 | tf_op jit(solution)/shard_map/all_gather | solution.py:108
  15.4 0.6 copy-start.10
  298.1 4.7 copy-start.5
  302.8 0.9 copy-start.2
  302.9 1.7 copy-start
  305.0 2.5 copy-start.3
  305.0 2.5 copy-start.4
  306.5 1.3 slice-start
  439.4 123.8 %copy-start.11 = (f32[128]{0:T(128)S(1)}, f32[128]{0:T(128)}, u32[]{:S(2)}) copy-start(f32[128]{0:T(128)} %copy-done.10) | copy-start | bytes 1540
  442.7 122.8 %copy-start.6 = (bf16[1,128,256]{2,1,0:T(8,128)(2,1)S(1)}, bf16[1,128,256]{2,1,0:T(8,128)(2,1)}, u32[]{:S(2)}) copy-start(bf16[1,128,256]{2,1,0:T(8,128)(2,1)} %param.13) | copy-start | bytes 196612
  442.7 122.8 %copy-start.9 = (f32[256]{0:T(256)S(1)}, f32[256]{0:T(256)}, u32[]{:S(2)}) copy-start(f32[256]{0:T(256)} %param.18) | copy-start | bytes 3076
  566.3 544.0 %all-reduce.31.cloned.1.call-start = ((), (), s32[]{:S(2)}) async-start(), calls=%async_computation.5 | async-start | bytes 262144 | tf_op jit(solution)/shard_map/psum | solution.py:112
  611.0 248.6 %copy-start.1 = (bf16[2048,512]{1,0:T(8,128)(2,1)S(1)}, bf16[2048,512]{1,0:T(8,128)(2,1)}, u32[]{:S(2)}) copy-start(bf16[2048,512]{1,0:T(8,128)(2,1)} %all-gather.6.cloned.1.call-done) | copy-start | bytes 6291460
  859.5 249.5 %copy-start.7 = (f32[4,256]{1,0:T(4,128)S(1)}, f32[4,256]{1,0:T(4,128)}, u32[]{:S(2)}) copy-start(f32[4,256]{1,0:T(4,128)} %param.17) | copy-start | bytes 12292
  859.5 249.5 %copy-start.8 = (f32[4,256]{1,0:T(4,128)S(1)}, f32[4,256]{1,0:T(4,128)}, u32[]{:S(2)}) copy-start(f32[4,256]{1,0:T(4,128)} %param.16) | copy-start | bytes 12292
  859.6 252.3 %reduce-scatter.2.cloned.1.call-start = ((), (), s32[]{:S(2)}) async-start(), calls=%async_computation.3 | async-start | bytes 589824 | tf_op jit(solution)/shard_map/reduce_scatter | solution.py:101
Sparse Core Ops, SparseCore 0:
  10.6 210.3 all-gather.5
  566.4 289.3 all-gather.7
  859.7 59.0 all-reduce.30
  923.7 110.6 reduce-scatter.1
where the time goes:
time: 1120 us
  blocking collectives  772 us (69%)
  waiting for transfers between devices  245 us (22%)
  other arithmetic  40.2 us (4%)
  local copies, waits for them, and re-layouts  38.6 us (3%)
  between operations  15 us (1%)
    all_gather x4, blocking collectives, carried_in(): gathered = jax.tree.map(lambda a: lax.all_gather(a, axis), part)  420 us
    psum x1, blocking collectives, body(): lax.psum((skip_part, paired_part, carried_part), ('dp', 'ctx'))  248 us
    all_gather x1, waiting for transfers between devices, body(): lax.all_gather(cot_both, 'ctx', axis=0, tiled=True)  245 us
    all_gather x1, blocking collectives, body(): feats = lax.all_gather(flat, 'tensor', axis=1, tiled=True)  59.5 us
    all_to_all x1, blocking collectives, body(): lax.all_to_all(feats, 'ctx', split_axis=1, concat_axis=0, tiled=True)  44.6 us
    pad x12, local copies, waits for them, and re-layouts, body(): local = lax.associative_scan(link, (keep, drive), axis=1)[1]  24.6 us
    add x42, other arithmetic, link(): return (first[0] * second[0], second[0] * first[1] + second[1])  23.3 us
  transfers between devices with their start and end apart: 4, of which 1 were waited for; matrix products, arithmetic and copies ran while one was open for 1% of the time, Pallas kernels for 0%

commit v1 on v0

v1 whole, which is shorter than its diff:
```python
import jax
import jax.numpy as jnp
from jax import lax
from jax.experimental import pallas as pl
from jax.experimental.pallas import tpu as pltpu
from jax.sharding import PartitionSpec as P

MESH = pl.DeviceIdType.MESH
F32 = jnp.float32
BF = jnp.bfloat16
SPAN = 128
WID = 256
MODES = 4
LINE = 8 * SPAN
NSTAT = 9 * WID

RT, RZ, RX, RS, RF = 0, 8, 16, 20, 24
RE, REX, RC, RP, RPA = 25, 33, 37, 38, 42
RG, RM, RB, RQS, RQX, RQZ, RW2 = 43, 47, 51, 52, 53, 57, 65
NRECV = 66
NSEND = 96


def dot(a, b, dims):
    return lax.dot_general(a, b, (dims, ((), ())), preferred_element_type=F32)


def split(u):
    hi = u.astype(BF)
    lo = (u - hi.astype(F32)).astype(BF)
    return hi, lo


def kernel(
    tok, cot, wv, wg, rate, resid, skip, clen,
    out, gtok, gwv, gwg, gskip, gres, grate,
    fown, fsib, wb, cbuf, ep, em, sloc, bloc, sb, zb, xsb, xb,
    cb, cs, pout, pin, pa_out, pa_in, gout, gin, mout, min_, bout, bin_, gfin,
    stq, stx, stz, ssem, rsem, lsem,
):
    d = lax.axis_index("dp")
    c = lax.axis_index("ctx")
    t = lax.axis_index("tensor")
    x, zl = c // 8, c % 8
    zh, y = t // 4, t % 4
    half, mate = zl // 4, zl % 4

    sib = {"dp": 1 - d}
    anti = {"tensor": (1 - zh) * 4 + y}
    partner = {"ctx": x * 8 + (1 - half) * 4 + mate}
    ys = [lax.rem(y + i, 4) for i in (1, 2, 3)]
    xs = [lax.rem(x + i, 4) for i in (1, 2, 3)]
    zs = [lax.rem(zl + i, 8) for i in range(1, 8)]
    ms = [lax.rem(mate + i, 4) for i in (1, 2, 3)]

    def ydev(k):
        return {"tensor": zh * 4 + k}

    def xdev(k):
        return {"ctx": k * 8 + zl}

    def zdev(k):
        return {"ctx": x * 8 + k}

    def mdev(k):
        return {"ctx": x * 8 + half * 4 + k}

    loads = [
        pltpu.make_async_copy(tok.at[0], fown.at[t], lsem.at[0]),
        pltpu.make_async_copy(cot.at[0], cbuf, lsem.at[1]),
    ]
    for cp in loads:
        cp.start()

    @pl.when(d == 0)
    def _():
        pltpu.make_async_copy(wv, wb.at[0, c], lsem.at[2]).start()

    @pl.when(d == 1)
    def _():
        pltpu.make_async_copy(wg, wb.at[1, c], lsem.at[2]).start()

    barrier = pltpu.get_barrier_semaphore()
    peers = (
        [sib, anti]
        + [ydev(k) for k in ys]
        + [xdev(k) for k in xs]
        + [zdev(k) for k in zs]
    )
    for who in peers:
        pl.semaphore_signal(barrier, inc=1, device_id=who, device_id_type=MESH)

    first = c * SPAN
    starts = [jnp.int32(0)]
    for k in range(7):
        starts.append(starts[-1] + clen[0, k])

    def seg(pos):
        total = (pos >= starts[0]).astype(jnp.int32)
        for s in starts[1:]:
            total = total + (pos >= s).astype(jnp.int32)
        return total

    def row(a):
        return jnp.concatenate([a[m : m + 1, :] for m in range(MODES)], axis=1)

    rt = rate[...]
    factor = jnp.sqrt(one_minus_exp(2.0 * rt))
    wm = resid[...] * factor
    r1 = row(rt)
    tcol = lax.broadcasted_iota(jnp.int32, (SPAN, WID), 0).astype(F32)
    for m in range(MODES):
        rm = rt[m : m + 1, :]
        ep[m] = jnp.exp(rm * tcol)
        em[m] = jnp.exp(-rm * tcol)
    ri = lax.broadcasted_iota(jnp.int32, (SPAN, SPAN), 0)
    ci = lax.broadcasted_iota(jnp.int32, (SPAN, SPAN), 1)
    sr, sc = seg(first + ri), seg(first + ci)
    lower = jnp.where((sr == sc) & (ci <= ri), 1.0, 0.0).astype(BF)
    upper = jnp.where((sr == sc) & (ci >= ri), 1.0, 0.0).astype(BF)
    seg_prev, seg_next = seg(first - 1), seg(first + SPAN)
    stc = seg(first + lax.broadcasted_iota(jnp.int32, (SPAN, WID), 0))
    clearf = jnp.where(stc == seg_prev, 1.0, 0.0)
    clearb = jnp.where(stc == seg_next, 1.0, 0.0)

    k8 = lax.broadcasted_iota(jnp.int32, (8, MODES * WID), 0)
    k4 = lax.broadcasted_iota(jnp.int32, (4, MODES * WID), 0)

    def weight(ok, dist):
        return jnp.where(ok, jnp.exp(-r1 * jnp.maximum(dist, 0).astype(F32)), 0.0)

    base = x * LINE
    endpos = base + SPAN * k8 + (SPAN - 1)
    topos = base + SPAN * k8
    seg_end, seg_top = seg(endpos), seg(topos)
    w_tot_f = weight(seg_end == seg(base + LINE - 1), base + LINE - 1 - endpos)
    w_tot_b = weight(seg_top == seg(base), topos - base)
    w_in_f = weight((k8 < zl) & (seg_end == seg_prev), first - 1 - endpos)
    w_in_b = weight((k8 > zl) & (seg_top == seg_next), topos - (first + SPAN))
    xend = (k4 + 1) * LINE - 1
    xtop = k4 * LINE
    w_x_f = weight((k4 < x) & (seg(xend) == seg_prev), first - 1 - xend)
    w_x_b = weight((k4 > x) & (seg(xtop) == seg_next), xtop - (first + SPAN))

    sends = []

    def send(src, dst, recv, who):
        cp = pltpu.make_async_remote_copy(
            src_ref=src,
            dst_ref=dst,
            send_sem=ssem.at[len(sends)],
            recv_sem=rsem.at[recv],
            device_id=who,
            device_id_type=MESH,
        )
        cp.start()
        sends.append(cp)

    def arrived(ref, recv):
        pltpu.make_async_copy(ref, ref, rsem.at[recv]).wait()

    for cp in loads:
        cp.wait()
    pltpu.make_async_copy(wv, wb.at[d, c], lsem.at[2]).wait()
    pl.semaphore_wait(barrier, len(peers))

    def spread_x(k):
        for i in xs:
            send(wb.at[d, x * 8 + k], wb.at[d, x * 8 + k], RX + x, xdev(i))

    send(fown.at[t], fown.at[t], RT + t, anti)
    send(wb.at[d, c], wb.at[d, c], RZ + zl, partner)
    for i in ms:
        send(wb.at[d, c], wb.at[d, c], RZ + zl, mdev(i))
    spread_x(zl)
    for i in ys:
        send(fown.at[t], fown.at[t], RT + t, ydev(i))
    for i in ms:
        k = half * 4 + i
        arrived(wb.at[d, x * 8 + k], RZ + k)
        spread_x(k)
    k = (1 - half) * 4 + mate
    arrived(wb.at[d, x * 8 + k], RZ + k)
    for i in ms:
        send(wb.at[d, x * 8 + k], wb.at[d, x * 8 + k], RZ + k, mdev(i))
    spread_x(k)
    ta = (1 - zh) * 4 + y
    arrived(fown.at[ta], RT + ta)
    for i in ys:
        send(fown.at[ta], fown.at[ta], RT + ta, ydev(i))
    for i in ms:
        k = (1 - half) * 4 + i
        arrived(wb.at[d, x * 8 + k], RZ + k)
        spread_x(k)

    def line(core, k):
        return wb.at[core, pl.ds(k * 8, 8)]

    send(line(d, x), line(d, x), RS + x, sib)
    for i in ys:
        arrived(fown.at[zh * 4 + i], RT + zh * 4 + i)
    for i in ys:
        arrived(fown.at[(1 - zh) * 4 + i], RT + (1 - zh) * 4 + i)
    send(fown, fsib, RF, sib)
    for i in (xs[0], xs[2], xs[1]):
        arrived(line(d, i), RX + i)
        send(line(d, i), line(d, i), RS + i, sib)
    for i in range(4):
        arrived(line(1 - d, i), RS + i)

    def wblock(core, j):
        return wb[core, 4 * j : 4 * j + 4].reshape(WID, WID)

    mm = ((1,), (0,))
    value = dot(fown[0], wblock(0, 0), mm)
    gate = dot(fown[0], wblock(1, 0), mm)
    for j in range(1, 8):
        value = value + dot(fown[j], wblock(0, j), mm)
        gate = gate + dot(fown[j], wblock(1, j), mm)
    upstream = cbuf[...].astype(F32)
    gm = upstream * gate

    for m in range(MODES):
        hi, lo = split(value * ep[m])
        s = dot(lower, hi, mm) + dot(lower, lo, mm)
        sloc[m] = s
        sb[0:1, m * WID : (m + 1) * WID] = s[SPAN - 1 :, :] * em[m, SPAN - 1 :, :]
        hi, lo = split(gm * wm[m : m + 1, :] * em[m])
        b = dot(upper, hi, mm) + dot(upper, lo, mm)
        bloc[m] = b
        sb[1:2, m * WID : (m + 1) * WID] = b[0:1, :]
    zb[zl] = sb[...]
    for i in (zs[6], zs[0], zs[5], zs[1], zs[4], zs[2], zs[3]):
        send(sb, zb.at[zl], RE + zl, zdev(i))
    for i in zs:
        arrived(zb.at[i], RE + i)
    fz, bz = zb[:, 0, :], zb[:, 1, :]
    xsb[0:1, :] = jnp.sum(w_tot_f * fz, axis=0, keepdims=True)
    xsb[1:2, :] = jnp.sum(w_tot_b * bz, axis=0, keepdims=True)
    xb[x] = xsb[...]
    for i in xs:
        send(xsb, xb.at[x], REX + x, xdev(i))
    inc_f = jnp.sum(w_in_f * fz, axis=0, keepdims=True)
    inc_b = jnp.sum(w_in_b * bz, axis=0, keepdims=True)
    for i in xs:
        arrived(xb.at[i], REX + i)
    inc_f = inc_f + jnp.sum(w_x_f * xb[:, 0, :], axis=0, keepdims=True)
    inc_b = inc_b + jnp.sum(w_x_b * xb[:, 1, :], axis=0, keepdims=True)
    inc_f = inc_f * jnp.exp(-r1)
    inc_b = inc_b * jnp.exp(-float(SPAN) * r1)

    sk = skip[...]
    mixed = sk * value
    gval = sk * gm
    stq[d, :, 0:WID] = jnp.sum(gm * value, axis=0, keepdims=True)
    for m in range(MODES):
        lanes = slice(m * WID, (m + 1) * WID)
        state = em[m] * (sloc[m] + clearf * inc_f[:, lanes])
        gst = ep[m] * (bloc[m] + clearb * inc_b[:, lanes])
        mixed = mixed + wm[m : m + 1, :] * state
        gval = gval + gst
        lo = WID * (1 + m)
        stq[d, :, lo : lo + WID] = jnp.sum(gm * state, axis=0, keepdims=True)
        lo = WID * (5 + m)
        stq[d, :, lo : lo + WID] = jnp.sum(gst * (state - value), axis=0, keepdims=True)
    out[0] = (gate * mixed).astype(BF)
    cv = gval.astype(BF)
    cg = (upstream * mixed).astype(BF)
    cb[0] = cv
    cb[1] = cg
    send(cb.at[1 - d], cs, RC, sib)
    send(stq.at[d], stq.at[d], RQS, sib)

    nt = ((1,), (1,))

    def share(j):
        wj = wb[:, pl.ds(4 * j, 4)]
        return dot(cv, wj[0].reshape(WID, WID), nt) + dot(cg, wj[1].reshape(WID, WID), nt)

    for i in (ys[1], ys[0], ys[2]):
        for h in range(2):
            pout[i, h] = share(h * 4 + i).astype(BF)
        send(pout.at[i], pin.at[y], RP + y, ydev(i))
    for h in range(2):
        pin[y, h] = share(h * 4 + y).astype(BF)

    tn = ((0,), (0,))
    arrived(fsib, RF)
    arrived(cs, RC)
    mine, theirs = cb[d], cs[...]

    def slab(j):
        g = dot(fown[j], mine, tn) + dot(fsib[j], theirs, tn)
        return g.reshape(4, 64, WID)

    for i in (xs[1], xs[0], xs[2]):
        for h in range(2):
            gout[i, 4 * h : 4 * h + 4] = slab(2 * i + h).astype(BF)
        send(gout.at[i], gin.at[x], RG + x, xdev(i))
    own = [slab(2 * x + h) for h in range(2)]

    arrived(stq.at[1 - d], RQS)
    stx[x] = stq[0] + stq[1]
    for i in xs:
        send(stx.at[x], stx.at[x], RQX + x, xdev(i))

    for i in ys:
        arrived(pin.at[i], RP + i)
    other = pin[0, 1 - zh].astype(F32)
    for k in range(1, 4):
        other = other + pin[k, 1 - zh].astype(F32)
    pa_out[...] = other.astype(BF)
    send(pa_out, pa_in, RPA, anti)
    kept = pin[0, zh].astype(F32)
    for k in range(1, 4):
        kept = kept + pin[k, zh].astype(F32)

    for i in xs:
        arrived(stx.at[i], RQX + i)
    stz[zl] = (stx[0] + stx[1]) + (stx[2] + stx[3])
    for i in zs:
        send(stz.at[zl], stz.at[zl], RQZ + zl, zdev(i))

    for i in xs:
        arrived(gin.at[i], RG + i)
    for h in range(2):
        g = own[h]
        for i in xs:
            g = g + gin[i, 4 * h : 4 * h + 4].astype(F32)
        mout[:, h] = g.astype(BF)
    for i in ms:
        send(mout.at[i], min_.at[mate], RM + mate, mdev(i))
    for i in ms:
        arrived(min_.at[i], RM + i)

    def summed(h):
        g = mout[mate, h].astype(F32)
        for i in ms:
            g = g + min_[i, h].astype(F32)
        return g

    bout[...] = summed(1 - half).astype(BF)
    send(bout, bin_, RB, partner)
    g = summed(half)

    for i in zs:
        arrived(stz.at[i], RQZ + i)
    tot = stz[0]
    for k in range(1, 8):
        tot = tot + stz[k]
    gskip[...] = tot[:, 0:WID]
    ratio = resid[...] * jnp.exp(-2.0 * rt) / factor
    for m in range(MODES):
        paired = tot[:, WID * (1 + m) : WID * (2 + m)]
        carried = tot[:, WID * (5 + m) : WID * (6 + m)]
        gres[m : m + 1, :] = factor[m : m + 1, :] * paired
        grate[m : m + 1, :] = ratio[m : m + 1, :] * paired - carried

    arrived(bin_, RB)
    gfin[d] = g + bin_[...].astype(F32)
    send(gfin.at[d], gfin.at[d], RW2, sib)
    arrived(pa_in, RPA)
    gtok[0] = (kept + pa_in[...].astype(F32)).astype(BF)
    arrived(gfin.at[1 - d], RW2)
    gwv[...] = gfin[0]
    gwg[...] = gfin[1]
    for cp in sends:
        cp.wait_send()


def one_minus_exp(a):
    term = a
    total = a
    for k in range(2, 8):
        term = term * (-a / k)
        total = total + term
    return total


def body(tokens, cotangent, w_value, w_gate, decay_rate, residue, skip_gain, contig_len):
    vm = pl.BlockSpec(memory_space=pltpu.VMEM)
    hbm = pl.BlockSpec(memory_space=pl.ANY)
    smem = pl.BlockSpec(memory_space=pltpu.SMEM)
    sds = jax.ShapeDtypeStruct
    outs = pl.pallas_call(
        kernel,
        out_shape=(
            sds((1, SPAN, WID), BF),
            sds((1, SPAN, WID), BF),
            sds((64, WID), F32),
            sds((64, WID), F32),
            sds((1, WID), F32),
            sds((MODES, WID), F32),
            sds((MODES, WID), F32),
        ),
        in_specs=[hbm, hbm, hbm, hbm, vm, vm, vm, smem],
        out_specs=(vm,) * 7,
        scratch_shapes=[
            pltpu.VMEM((8, SPAN, WID), BF),
            pltpu.VMEM((8, SPAN, WID), BF),
            pltpu.VMEM((2, 32, 64, WID), BF),
            pltpu.VMEM((SPAN, WID), BF),
            pltpu.VMEM((MODES, SPAN, WID), F32),
            pltpu.VMEM((MODES, SPAN, WID), F32),
            pltpu.VMEM((MODES, SPAN, WID), F32),
            pltpu.VMEM((MODES, SPAN, WID), F32),
            pltpu.VMEM((2, MODES * WID), F32),
            pltpu.VMEM((8, 2, MODES * WID), F32),
            pltpu.VMEM((2, MODES * WID), F32),
            pltpu.VMEM((4, 2, MODES * WID), F32),
            pltpu.VMEM((2, SPAN, WID), BF),
            pltpu.VMEM((SPAN, WID), BF),
            pltpu.VMEM((4, 2, SPAN, WID), BF),
            pltpu.VMEM((4, 2, SPAN, WID), BF),
            pltpu.VMEM((SPAN, WID), BF),
            pltpu.VMEM((SPAN, WID), BF),
            pltpu.VMEM((4, 8, 64, WID), BF),
            pltpu.VMEM((4, 8, 64, WID), BF),
            pltpu.VMEM((4, 2, 64, WID), BF),
            pltpu.VMEM((4, 2, 64, WID), BF),
            pltpu.VMEM((64, WID), BF),
            pltpu.VMEM((64, WID), BF),
            pltpu.VMEM((2, 64, WID), F32),
            pltpu.VMEM((2, 1, NSTAT), F32),
            pltpu.VMEM((4, 1, NSTAT), F32),
            pltpu.VMEM((8, 1, NSTAT), F32),
            pltpu.SemaphoreType.DMA((NSEND,)),
            pltpu.SemaphoreType.DMA((NRECV,)),
            pltpu.SemaphoreType.DMA((3,)),
        ],
        compiler_params=pltpu.CompilerParams(
            collective_id=0, has_side_effects=True, vmem_limit_bytes=48 << 20
        ),
        name="step",
    )(
        tokens, cotangent, w_value, w_gate, decay_rate, residue,
        skip_gain.reshape(1, WID), contig_len,
    )
    outs = list(outs)
    outs[4] = outs[4].reshape(WID)
    return tuple(outs)


def solution(mesh):
    in_specs = (
        P("dp", "ctx", "tensor"),
        P("dp", "ctx", "tensor"),
        P("ctx", "tensor"),
        P("ctx", "tensor"),
        P(None, "tensor"),
        P(None, "tensor"),
        P("tensor"),
        P("dp", None),
    )
    out_specs = (
        P("dp", "ctx", "tensor"),
        P("dp", "ctx", "tensor"),
        P("ctx", "tensor"),
        P("ctx", "tensor"),
        P("tensor"),
        P(None, "tensor"),
        P(None, "tensor"),
    )
    return jax.shard_map(body, mesh=mesh, in_specs=in_specs, out_specs=out_specs, check_vma=False)
```

time: 1120 us -> 95.3 us (0.09)
  blocking collectives: 772 us -> 0 us
  waiting for transfers between devices: 245 us -> 0 us
  Pallas kernels: 0 us -> 84.7 us
  other arithmetic: 40.2 us -> 0 us
  local copies, waits for them, and re-layouts: 38.6 us -> 9.51 us
  between operations: 15 us -> 0.67 us
    all_gather x5 -> x0, blocking collectives: 480 us -> none  [the longest x4 420 us: carried_in(): gathered = jax.tree.map(lambda a: lax.all_gather(a, axis), part)]
    psum x1 -> x0, blocking collectives: 248 us -> none  [body(): lax.psum((skip_part, paired_part, carried_part), ('dp', 'ctx'))]
    all_gather x2 -> x0, waiting for transfers between devices: 245 us -> none  [the longest x1 245 us: body(): lax.all_gather(cot_both, 'ctx', axis=0, tiled=True)]
    pallas_call x0 -> x1, Pallas kernels: none -> 84.7 us  [body(): pl.pallas_call(kernel, out_shape=(sds((1, SPAN, WID), BF), sds((1, SPAN,...]
    all_to_all x1 -> x0, blocking collectives: 44.6 us -> none  [body(): lax.all_to_all(feats, 'ctx', split_axis=1, concat_axis=0, tiled=True)]
    pad x24 -> x0, local copies, waits for them, and re-layouts: 28 us -> none  [the longest x12 24.6 us: body(): local = lax.associative_scan(link, (keep, drive), axis=1)[1]]
    add x59 -> x0, other arithmetic: 25.7 us -> none  [the longest x42 23.3 us: link(): return (first[0] * second[0], second[0] * first[1] + second[1])]
  transfers between devices with their start and end apart: 4 -> 0, of which waited for: 1 -> 0; matrix products, arithmetic and copies ran while one was open for 1% -> 0% of each run, Pallas kernels for 0% -> 0%
where the time goes in v1:
time: 95.3 us; the launch traced here: 94.9 us
  Pallas kernels  84.7 us (89%)
  local copies, waits for them, and re-layouts  9.51 us (10%)
    pallas_call x1, Pallas kernels, body(): pl.pallas_call(kernel, out_shape=(sds((1, SPAN, WID), BF), sds((1, SPAN,...  84.7 us
    unnamed x23, local copies, waits for them, and re-layouts  9.51 us

profile of v1, /device:TPU:1, one launch (start us, length us, event | category | flops | bytes accessed | tf_op | source)
XLA Modules:
  0.0 94.9 jit_solution(15554299384859694406)
XLA Ops:
  0.6 0.0 copy-start.7
  0.6 0.0 copy-start.6
  0.7 0.6 copy-done.7
  1.3 0.0 copy-done.6
  1.3 0.0 copy-start
  1.3 0.8 copy-done
  2.2 0.0 copy-start.1
  2.2 0.8 copy-done.1
  3.0 0.0 copy-start.2
  3.0 0.8 copy-done.2
  3.8 0.0 copy-start.3
  3.8 0.8 copy-done.3
  4.5 0.0 copy-start.4
  4.5 0.7 copy-done.4
  5.2 0.0 copy-start.5
  5.2 0.7 copy-done.5
  5.9 84.7 %step.1 = (bf16[1,128,256]{2,1,0:T(8,128)(2,1)S(1)}, bf16[1,128,256]{2,1,0:T(8,128)(2,1)S(1)}, f32[64,256]{1,0:T(8,128)S(1)}, f32[64,256]{1,0:T(8,128)S(1)}, f32...) custom-call(bf16[1,128,256]{2,1,0:T(8,128)(2,1)S(1)} %copy-done, ...), custom_call_target="tpu_custom_call" | custom-call | tf_op jit(solution)/shard_map/step/pallas_call | solution.py:385
  90.6 0.6 copy.22
  91.2 0.6 copy.23
  91.9 0.6 copy.24
  92.5 0.6 copy.25
  93.1 0.6 copy.26
  93.7 0.6 copy.27
  94.3 0.6 copy.28
Async XLA Ops:
  0.6 0.7 copy-start.7
  0.6 0.7 copy-start.6
  1.3 0.8 copy-start
  2.2 0.8 copy-start.1
  3.0 0.8 copy-start.2
  3.8 0.8 copy-start.3
  4.5 0.7 copy-start.4
  5.2 0.7 copy-start.5

commit v2 on v1

--- a/solution.py
+++ b/solution.py
@@ -14,11 +14,11 @@
 LINE = 8 * SPAN
 NSTAT = 9 * WID
 
-RT, RZ, RX, RS, RF = 0, 8, 16, 20, 24
-RE, REX, RC, RP, RPA = 25, 33, 37, 38, 42
-RG, RM, RB, RQS, RQX, RQZ, RW2 = 43, 47, 51, 52, 53, 57, 65
-NRECV = 66
-NSEND = 96
+RT, RZ, RX, RS, RF = 0, 8, 16, 24, 32
+RE, REX, RC, RP, RPA = 33, 41, 45, 46, 54
+RG, RM, RB, RQS, RQX, RQZ, RW2 = 55, 63, 71, 72, 73, 77, 85
+NRECV = 86
+NSEND = 104
 
 
 def dot(a, b, dims):
@@ -32,11 +32,11 @@
 
 
 def kernel(
-    tok, cot, wv, wg, rate, resid, skip, clen,
+    tok, cot, wv, wg, rate_h, resid_h, skip_h, clen_h,
     out, gtok, gwv, gwg, gskip, gres, grate,
     fown, fsib, wb, cbuf, ep, em, sloc, bloc, sb, zb, xsb, xb,
-    cb, cs, pout, pin, pa_out, pa_in, gout, gin, mout, min_, bout, bin_, gfin,
-    stq, stx, stz, ssem, rsem, lsem,
+    cb, cs, pout, pin, pa_out, pa_in, gout, gin, gown, mout, min_, bout, bin_, gfin,
+    wt, ft, stq, stx, stz, rate, resid, skip, clen, ssem, rsem, lsem,
 ):
     d = lax.axis_index("dp")
     c = lax.axis_index("ctx")
@@ -69,7 +69,13 @@
         pltpu.make_async_copy(tok.at[0], fown.at[t], lsem.at[0]),
         pltpu.make_async_copy(cot.at[0], cbuf, lsem.at[1]),
     ]
-    for cp in loads:
+    small = [
+        pltpu.make_async_copy(rate_h, rate, lsem.at[3]),
+        pltpu.make_async_copy(resid_h, resid, lsem.at[4]),
+        pltpu.make_async_copy(skip_h, skip, lsem.at[5]),
+        pltpu.make_async_copy(clen_h, clen, lsem.at[6]),
+    ]
+    for cp in small + loads:
         cp.start()
 
     @pl.when(d == 0)
@@ -90,6 +96,8 @@
     for who in peers:
         pl.semaphore_signal(barrier, inc=1, device_id=who, device_id_type=MESH)
 
+    for cp in small:
+        cp.wait()
     first = c * SPAN
     starts = [jnp.int32(0)]
     for k in range(7):
@@ -165,23 +173,31 @@
     pl.semaphore_wait(barrier, len(peers))
 
     def spread_x(k):
-        for i in xs:
-            send(wb.at[d, x * 8 + k], wb.at[d, x * 8 + k], RX + x, xdev(i))
-
+        for i in (xs[1], xs[0], xs[2]):
+            send(wb.at[d, x * 8 + k], wb.at[d, x * 8 + k], RX + 2 * x + k // 4, xdev(i))
+
+    def quad(core, k, g):
+        return wb.at[core, pl.ds(k * 8 + 4 * g, 4)]
+
+    def to_sib(k, g):
+        send(quad(d, k, g), quad(d, k, g), RS + 2 * k + g, sib)
+
+    near, far = half, 1 - half
+    for i in (ms[1], ms[0], ms[2]):
+        send(wb.at[d, c], wb.at[d, c], RZ + zl, mdev(i))
+    send(wb.at[d, c], wb.at[d, c], RZ + zl, partner)
     send(fown.at[t], fown.at[t], RT + t, anti)
-    send(wb.at[d, c], wb.at[d, c], RZ + zl, partner)
-    for i in ms:
-        send(wb.at[d, c], wb.at[d, c], RZ + zl, mdev(i))
     spread_x(zl)
     for i in ys:
         send(fown.at[t], fown.at[t], RT + t, ydev(i))
     for i in ms:
-        k = half * 4 + i
+        k = near * 4 + i
         arrived(wb.at[d, x * 8 + k], RZ + k)
         spread_x(k)
-    k = (1 - half) * 4 + mate
+    to_sib(x, near)
+    k = far * 4 + mate
     arrived(wb.at[d, x * 8 + k], RZ + k)
-    for i in ms:
+    for i in (ms[1], ms[0], ms[2]):
         send(wb.at[d, x * 8 + k], wb.at[d, x * 8 + k], RZ + k, mdev(i))
     spread_x(k)
     ta = (1 - zh) * 4 + y
@@ -189,24 +205,24 @@
     for i in ys:
         send(fown.at[ta], fown.at[ta], RT + ta, ydev(i))
     for i in ms:
-        k = (1 - half) * 4 + i
+        k = far * 4 + i
         arrived(wb.at[d, x * 8 + k], RZ + k)
         spread_x(k)
-
-    def line(core, k):
-        return wb.at[core, pl.ds(k * 8, 8)]
-
-    send(line(d, x), line(d, x), RS + x, sib)
+    to_sib(x, far)
+    for i in (xs[0], xs[2], xs[1]):
+        arrived(quad(d, i, near), RX + 2 * i + near)
+        to_sib(i, near)
     for i in ys:
         arrived(fown.at[zh * 4 + i], RT + zh * 4 + i)
     for i in ys:
         arrived(fown.at[(1 - zh) * 4 + i], RT + (1 - zh) * 4 + i)
+    for i in (xs[0], xs[2], xs[1]):
+        arrived(quad(d, i, far), RX + 2 * i + far)
+        to_sib(i, far)
     send(fown, fsib, RF, sib)
-    for i in (xs[0], xs[2], xs[1]):
-        arrived(line(d, i), RX + i)
-        send(line(d, i), line(d, i), RS + i, sib)
     for i in range(4):
-        arrived(line(1 - d, i), RS + i)
+        for g in range(2):
+            arrived(quad(1 - d, i, g), RS + 2 * i + g)
 
     def wblock(core, j):
         return wb[core, 4 * j : 4 * j + 4].reshape(WID, WID)
@@ -232,6 +248,12 @@
     zb[zl] = sb[...]
     for i in (zs[6], zs[0], zs[5], zs[1], zs[4], zs[2], zs[3]):
         send(sb, zb.at[zl], RE + zl, zdev(i))
+    arrived(fsib, RF)
+    for j in range(8):
+        wt[j, 0:WID] = wblock(0, j).T
+        wt[j, WID:] = wblock(1, j).T
+        ft[j, :, 0:SPAN] = fown[j].T
+        ft[j, :, SPAN:] = fsib[j].T
     for i in zs:
         arrived(zb.at[i], RE + i)
     fz, bz = zb[:, 0, :], zb[:, 1, :]
@@ -271,77 +293,75 @@
     send(cb.at[1 - d], cs, RC, sib)
     send(stq.at[d], stq.at[d], RQS, sib)
 
-    nt = ((1,), (1,))
-
-    def share(j):
-        wj = wb[:, pl.ds(4 * j, 4)]
-        return dot(cv, wj[0].reshape(WID, WID), nt) + dot(cg, wj[1].reshape(WID, WID), nt)
-
-    for i in (ys[1], ys[0], ys[2]):
-        for h in range(2):
-            pout[i, h] = share(h * 4 + i).astype(BF)
-        send(pout.at[i], pin.at[y], RP + y, ydev(i))
-    for h in range(2):
-        pin[y, h] = share(h * 4 + y).astype(BF)
-
-    tn = ((0,), (0,))
-    arrived(fsib, RF)
+    both = jnp.concatenate([cv, cg], axis=1)
+
+    def share(h, i):
+        return dot(both, wt[h * 4 + i], mm).astype(BF)
+
+    def shares(h):
+        for i in (ys[1], ys[0], ys[2]):
+            pout[h, i] = share(h, i)
+            send(pout.at[h, i], pin.at[h, y], RP + 4 * h + y, ydev(i))
+        pin[h, y] = share(h, y)
+
+    def shares_sum(h):
+        for i in ys:
+            arrived(pin.at[h, i], RP + 4 * h + i)
+        total = pin[h, 0].astype(F32)
+        for k in range(1, 4):
+            total = total + pin[h, k].astype(F32)
+        return total
+
+    def slab(cots, h, i):
+        return dot(ft[2 * i + h], cots, mm).reshape(4, 64, WID)
+
+    def slabs(cots, h):
+        for i in (xs[1], xs[0], xs[2]):
+            gout[h, i] = slab(cots, h, i).astype(BF)
+            send(gout.at[h, i], gin.at[h, x], RG + 4 * h + x, xdev(i))
+        gown[h] = slab(cots, h, x)
+
+    def slabs_sum(h):
+        for i in xs:
+            arrived(gin.at[h, i], RG + 4 * h + i)
+        g = gown[h]
+        for i in xs:
+            g = g + gin[h, i].astype(F32)
+        mout[h] = g.astype(BF)
+        for i in (ms[1], ms[0], ms[2]):
+            send(mout.at[h, i], min_.at[h, mate], RM + 4 * h + mate, mdev(i))
+
+    def mates_sum(h):
+        for i in ms:
+            arrived(min_.at[h, i], RM + 4 * h + i)
+        g = mout[h, mate].astype(F32)
+        for i in ms:
+            g = g + min_[h, i].astype(F32)
+        return g
+
+    shares(1 - zh)
     arrived(cs, RC)
-    mine, theirs = cb[d], cs[...]
-
-    def slab(j):
-        g = dot(fown[j], mine, tn) + dot(fsib[j], theirs, tn)
-        return g.reshape(4, 64, WID)
-
-    for i in (xs[1], xs[0], xs[2]):
-        for h in range(2):
-            gout[i, 4 * h : 4 * h + 4] = slab(2 * i + h).astype(BF)
-        send(gout.at[i], gin.at[x], RG + x, xdev(i))
-    own = [slab(2 * x + h) for h in range(2)]
-
+    cots = jnp.concatenate([cb[d], cs[...]], axis=0)
+    slabs(cots, far)
+    shares(zh)
+    slabs(cots, near)
     arrived(stq.at[1 - d], RQS)
     stx[x] = stq[0] + stq[1]
     for i in xs:
         send(stx.at[x], stx.at[x], RQX + x, xdev(i))
-
-    for i in ys:
-        arrived(pin.at[i], RP + i)
-    other = pin[0, 1 - zh].astype(F32)
-    for k in range(1, 4):
-        other = other + pin[k, 1 - zh].astype(F32)
-    pa_out[...] = other.astype(BF)
+    pa_out[...] = shares_sum(1 - zh).astype(BF)
     send(pa_out, pa_in, RPA, anti)
-    kept = pin[0, zh].astype(F32)
-    for k in range(1, 4):
-        kept = kept + pin[k, zh].astype(F32)
-
+    slabs_sum(far)
     for i in xs:
         arrived(stx.at[i], RQX + i)
     stz[zl] = (stx[0] + stx[1]) + (stx[2] + stx[3])
     for i in zs:
         send(stz.at[zl], stz.at[zl], RQZ + zl, zdev(i))
-
-    for i in xs:
-        arrived(gin.at[i], RG + i)
-    for h in range(2):
-        g = own[h]
-        for i in xs:
-            g = g + gin[i, 4 * h : 4 * h + 4].astype(F32)
-        mout[:, h] = g.astype(BF)
-    for i in ms:
-        send(mout.at[i], min_.at[mate], RM + mate, mdev(i))
-    for i in ms:
-        arrived(min_.at[i], RM + i)
-
-    def summed(h):
-        g = mout[mate, h].astype(F32)
-        for i in ms:
-            g = g + min_[i, h].astype(F32)
-        return g
-
-    bout[...] = summed(1 - half).astype(BF)
+    slabs_sum(near)
+    bout[...] = mates_sum(far).astype(BF)
     send(bout, bin_, RB, partner)
-    g = summed(half)
+    kept = shares_sum(zh)
+    g = mates_sum(near)
 
     for i in zs:
         arrived(stz.at[i], RQZ + i)
@@ -377,23 +397,32 @@
     return total
 
 
+def store(*refs):
+    sem = refs[14]
+    copies = [pltpu.make_async_copy(refs[k], refs[7 + k], sem.at[k]) for k in range(7)]
+    for cp in copies:
+        cp.start()
+    for cp in copies:
+        cp.wait()
+
+
 def body(tokens, cotangent, w_value, w_gate, decay_rate, residue, skip_gain, contig_len):
     vm = pl.BlockSpec(memory_space=pltpu.VMEM)
-    hbm = pl.BlockSpec(memory_space=pl.ANY)
-    smem = pl.BlockSpec(memory_space=pltpu.SMEM)
+    hbm = pl.BlockSpec(memory_space=pltpu.HBM)
     sds = jax.ShapeDtypeStruct
+    shapes = (
+        sds((1, SPAN, WID), BF),
+        sds((1, SPAN, WID), BF),
+        sds((64, WID), F32),
+        sds((64, WID), F32),
+        sds((1, WID), F32),
+        sds((MODES, WID), F32),
+        sds((MODES, WID), F32),
+    )
     outs = pl.pallas_call(
         kernel,
-        out_shape=(
-            sds((1, SPAN, WID), BF),
-            sds((1, SPAN, WID), BF),
-            sds((64, WID), F32),
-            sds((64, WID), F32),
-            sds((1, WID), F32),
-            sds((MODES, WID), F32),
-            sds((MODES, WID), F32),
-        ),
-        in_specs=[hbm, hbm, hbm, hbm, vm, vm, vm, smem],
+        out_shape=shapes,
+        in_specs=[hbm] * 8,
         out_specs=(vm,) * 7,
         scratch_shapes=[
             pltpu.VMEM((8, SPAN, WID), BF),
@@ -410,32 +439,47 @@
             pltpu.VMEM((4, 2, MODES * WID), F32),
             pltpu.VMEM((2, SPAN, WID), BF),
             pltpu.VMEM((SPAN, WID), BF),
-            pltpu.VMEM((4, 2, SPAN, WID), BF),
-            pltpu.VMEM((4, 2, SPAN, WID), BF),
+            pltpu.VMEM((2, 4, SPAN, WID), BF),
+            pltpu.VMEM((2, 4, SPAN, WID), BF),
             pltpu.VMEM((SPAN, WID), BF),
             pltpu.VMEM((SPAN, WID), BF),
-            pltpu.VMEM((4, 8, 64, WID), BF),
-            pltpu.VMEM((4, 8, 64, WID), BF),
-            pltpu.VMEM((4, 2, 64, WID), BF),
-            pltpu.VMEM((4, 2, 64, WID), BF),
+            pltpu.VMEM((2, 4, 4, 64, WID), BF),
+            pltpu.VMEM((2, 4, 4, 64, WID), BF),
+            pltpu.VMEM((2, 4, 64, WID), F32),
+            pltpu.VMEM((2, 4, 64, WID), BF),
+            pltpu.VMEM((2, 4, 64, WID), BF),
             pltpu.VMEM((64, WID), BF),
             pltpu.VMEM((64, WID), BF),
             pltpu.VMEM((2, 64, WID), F32),
+            pltpu.VMEM((8, 2 * WID, WID), BF),
+            pltpu.VMEM((8, WID, 2 * SPAN), BF),
             pltpu.VMEM((2, 1, NSTAT), F32),
             pltpu.VMEM((4, 1, NSTAT), F32),
             pltpu.VMEM((8, 1, NSTAT), F32),
+            pltpu.VMEM((MODES, WID), F32),
+            pltpu.VMEM((MODES, WID), F32),
+            pltpu.VMEM((1, WID), F32),
+            pltpu.SMEM((1, 8), jnp.int32),
             pltpu.SemaphoreType.DMA((NSEND,)),
             pltpu.SemaphoreType.DMA((NRECV,)),
-            pltpu.SemaphoreType.DMA((3,)),
+            pltpu.SemaphoreType.DMA((7,)),
         ],
         compiler_params=pltpu.CompilerParams(
-            collective_id=0, has_side_effects=True, vmem_limit_bytes=48 << 20
+            collective_id=0, has_side_effects=True, vmem_limit_bytes=67043328
         ),
         name="step",
     )(
         tokens, cotangent, w_value, w_gate, decay_rate, residue,
         skip_gain.reshape(1, WID), contig_len,
     )
+    outs = pl.pallas_call(
+        store,
+        out_shape=shapes,
+        in_specs=[vm] * 7,
+        out_specs=(hbm,) * 7,
+        scratch_shapes=[pltpu.SemaphoreType.DMA((7,))],
+        name="store",
+    )(*outs)
     outs = list(outs)
     outs[4] = outs[4].reshape(WID)
     return tuple(outs)

time: 95.3 us -> 82 us (0.86)
  local copies, waits for them, and re-layouts: 9.51 us -> 0 us
  Pallas kernels: 84.7 us -> 80.1 us
    unnamed x23 -> x0, local copies, waits for them, and re-layouts: 9.51 us -> none
    pallas_call x1 -> x2, Pallas kernels: 84.7 us -> 80.1 us  [the longest x1 78.4 us: body(): pl.pallas_call(kernel, out_shape=shapes, in_specs=[hbm] * 8, out_specs=(v...]
where the time goes in v2:
time: 82 us; the launch traced here: 80.8 us
  Pallas kernels  80.1 us (98%)
    pallas_call x1, Pallas kernels, body(): pl.pallas_call(kernel, out_shape=shapes, in_specs=[hbm] * 8, out_specs=(v...  78.4 us
    pallas_call x1, Pallas kernels, body(): pl.pallas_call(store, out_shape=shapes, in_specs=[vm] * 7, out_specs=(hbm...  1.71 us

profile of v2, /device:TPU:1, one launch (start us, length us, event | category | flops | bytes accessed | tf_op | source)
XLA Modules:
  0.0 80.8 jit_solution(5869081300389638697)
XLA Ops:
  0.6 78.4 %step.1 = (bf16[1,128,256]{2,1,0:T(8,128)(2,1)}, bf16[1,128,256]{2,1,0:T(8,128)(2,1)}, f32[64,256]{1,0:T(8,128)}, f32[64,256]{1,0:T(8,128)}, f32[1,256]{1,0:T(1,...) custom-call(bf16[1,128,256]{2,1,0:T(8,128)(2,1)} %tok.1, bf16[1,128,256]{2,1,0:T(8,128)(2,1)} %cot.1, bf16[64,256]{1,0:T(8,128)(2,1)} %wv.1, ...), custom_call_target="tpu_custom_call" | custom-call | tf_op jit(solution)/shard_map/step/pallas_call | solution.py:422
  79.1 1.7 %store.1 = (bf16[1,128,256]{2,1,0:T(8,128)(2,1)}, bf16[1,128,256]{2,1,0:T(8,128)(2,1)}, f32[64,256]{1,0:T(8,128)}, f32[64,256]{1,0:T(8,128)}, f32[1,256]{1,0:T(1...) custom-call(bf16[1,128,256]{2,1,0:T(8,128)(2,1)} %get-tuple-element.21.refs_0_, ...), custom_call_target="tpu_custom_call" | custom-call | tf_op jit(solution)/shard_map/store/pallas_call | solution.py:475

commit v3 on v2

--- a/solution.py
+++ b/solution.py
@@ -14,11 +14,12 @@
 LINE = 8 * SPAN
 NSTAT = 9 * WID
 
-RT, RZ, RX, RS, RF = 0, 8, 16, 24, 32
-RE, REX, RC, RP, RPA = 33, 41, 45, 46, 54
-RG, RM, RB, RQS, RQX, RQZ, RW2 = 55, 63, 71, 72, 73, 77, 85
-NRECV = 86
-NSEND = 104
+RT, RZ, RX, RS, RF = 0, 16, 24, 32, 40
+RE, REX, RC, RP, RPA = 41, 49, 53, 54, 62
+RG, RR, RM, RB, RW2 = 63, 71, 75, 83, 84
+RQS, RQX, RQM, RQP = 85, 86, 90, 94
+NRECV = 95
+NSEND = 128
 
 
 def dot(a, b, dims):
@@ -35,8 +36,8 @@
     tok, cot, wv, wg, rate_h, resid_h, skip_h, clen_h,
     out, gtok, gwv, gwg, gskip, gres, grate,
     fown, fsib, wb, cbuf, ep, em, sloc, bloc, sb, zb, xsb, xb,
-    cb, cs, pout, pin, pa_out, pa_in, gout, gin, gown, mout, min_, bout, bin_, gfin,
-    wt, ft, stq, stx, stz, rate, resid, skip, clen, ssem, rsem, lsem,
+    cb, cs, pout, pin, pa_out, pa_in, gr_out, gr_in, gk, gd, gc, gin, gown,
+    mout, min_, bout, bin_, gfin, wt, ft, stq, stx, stm, stp, rate, resid, skip, clen, ssem, rsem, lsem,
 ):
     d = lax.axis_index("dp")
     c = lax.axis_index("ctx")
@@ -183,13 +184,17 @@
         send(quad(d, k, g), quad(d, k, g), RS + 2 * k + g, sib)
 
     near, far = half, 1 - half
+    def piece(j, q):
+        return fown.at[j, pl.ds(q * (SPAN // 2), SPAN // 2)]
+
+    send(wb.at[d, c], wb.at[d, c], RZ + zl, partner)
     for i in (ms[1], ms[0], ms[2]):
         send(wb.at[d, c], wb.at[d, c], RZ + zl, mdev(i))
-    send(wb.at[d, c], wb.at[d, c], RZ + zl, partner)
-    send(fown.at[t], fown.at[t], RT + t, anti)
+    for q in range(2):
+        send(piece(t, q), piece(t, q), RT + 2 * t + q, anti)
     spread_x(zl)
     for i in ys:
-        send(fown.at[t], fown.at[t], RT + t, ydev(i))
+        send(fown.at[t], fown.at[t], RT + 2 * t, ydev(i))
     for i in ms:
         k = near * 4 + i
         arrived(wb.at[d, x * 8 + k], RZ + k)
@@ -200,22 +205,24 @@
     for i in (ms[1], ms[0], ms[2]):
         send(wb.at[d, x * 8 + k], wb.at[d, x * 8 + k], RZ + k, mdev(i))
     spread_x(k)
-    ta = (1 - zh) * 4 + y
-    arrived(fown.at[ta], RT + ta)
-    for i in ys:
-        send(fown.at[ta], fown.at[ta], RT + ta, ydev(i))
     for i in ms:
         k = far * 4 + i
         arrived(wb.at[d, x * 8 + k], RZ + k)
         spread_x(k)
     to_sib(x, far)
+    ta = (1 - zh) * 4 + y
+    for q in range(2):
+        arrived(piece(ta, q), RT + 2 * ta + q)
+        for i in ys:
+            send(piece(ta, q), piece(ta, q), RT + 2 * ta + q, ydev(i))
     for i in (xs[0], xs[2], xs[1]):
         arrived(quad(d, i, near), RX + 2 * i + near)
         to_sib(i, near)
     for i in ys:
-        arrived(fown.at[zh * 4 + i], RT + zh * 4 + i)
-    for i in ys:
-        arrived(fown.at[(1 - zh) * 4 + i], RT + (1 - zh) * 4 + i)
+        arrived(fown.at[zh * 4 + i], RT + 2 * (zh * 4 + i))
+    for q in range(2):
+        for i in ys:
+            arrived(piece((1 - zh) * 4 + i, q), RT + 2 * ((1 - zh) * 4 + i) + q)
     for i in (xs[0], xs[2], xs[1]):
         arrived(quad(d, i, far), RX + 2 * i + far)
         to_sib(i, far)
@@ -312,22 +319,42 @@
             total = total + pin[h, k].astype(F32)
         return total
 
-    def slab(cots, h, i):
+    right, left = xs[0], xs[2]
+
+    def slab(h, i):
         return dot(ft[2 * i + h], cots, mm).reshape(4, 64, WID)
 
-    def slabs(cots, h):
-        for i in (xs[1], xs[0], xs[2]):
-            gout[h, i] = slab(cots, h, i).astype(BF)
-            send(gout.at[h, i], gin.at[h, x], RG + 4 * h + x, xdev(i))
-        gown[h] = slab(cots, h, x)
-
-    def slabs_sum(h):
-        for i in xs:
-            arrived(gin.at[h, i], RG + 4 * h + i)
-        g = gown[h]
-        for i in xs:
-            g = g + gin[h, i].astype(F32)
-        mout[h] = g.astype(BF)
+    def x_start(h):
+        g = slab(h, xs[1]).astype(BF)
+        gr_out[h, 0] = g[0:2]
+        send(gr_out.at[h, 0], gr_in.at[h, 0], RR + 2 * h, xdev(right))
+        gr_out[h, 1] = g[2:4]
+        send(gr_out.at[h, 1], gr_in.at[h, 1], RR + 2 * h + 1, xdev(left))
+
+    def x_direct(h):
+        g = slab(h, right)
+        gk[h, 0] = g[0:2]
+        gd[h, 0] = g[2:4].astype(BF)
+        send(gd.at[h, 0], gin.at[h, 0, 1], RG + 4 * h + 1, xdev(right))
+        g = slab(h, left)
+        gk[h, 1] = g[2:4]
+        gd[h, 1] = g[0:2].astype(BF)
+        send(gd.at[h, 1], gin.at[h, 1, 0], RG + 4 * h + 2, xdev(left))
+
+    def x_relay(h):
+        for side, who, part in ((0, right, 0), (1, left, 1)):
+            arrived(gr_in.at[h, side], RR + 2 * h + side)
+            gc[h, side] = (gk[h, side] + gr_in[h, side].astype(F32)).astype(BF)
+            send(gc.at[h, side], gin.at[h, side, part], RG + 4 * h + 3 * side, xdev(who))
+
+    def x_sum(h):
+        for side in range(2):
+            for part in range(2):
+                arrived(gin.at[h, side, part], RG + 4 * h + 2 * side + part)
+        for part in range(2):
+            g = gown[h, 2 * part : 2 * part + 2]
+            g = g + gin[h, 0, part].astype(F32) + gin[h, 1, part].astype(F32)
+            mout[h, 2 * part : 2 * part + 2] = g.astype(BF)
         for i in (ms[1], ms[0], ms[2]):
             send(mout.at[h, i], min_.at[h, mate], RM + 4 * h + mate, mdev(i))
 
@@ -340,34 +367,39 @@
         return g
 
     shares(1 - zh)
-    arrived(cs, RC)
-    cots = jnp.concatenate([cb[d], cs[...]], axis=0)
-    slabs(cots, far)
-    shares(zh)
-    slabs(cots, near)
     arrived(stq.at[1 - d], RQS)
     stx[x] = stq[0] + stq[1]
     for i in xs:
         send(stx.at[x], stx.at[x], RQX + x, xdev(i))
+    arrived(cs, RC)
+    cots = jnp.concatenate([cb[d], cs[...]], axis=0)
+    x_start(far)
+    x_direct(far)
+    x_start(near)
+    shares(zh)
+    for h in (far, near):
+        gown[h] = slab(h, x)
+    x_relay(far)
+    x_direct(near)
     pa_out[...] = shares_sum(1 - zh).astype(BF)
     send(pa_out, pa_in, RPA, anti)
-    slabs_sum(far)
+    x_relay(near)
     for i in xs:
         arrived(stx.at[i], RQX + i)
-    stz[zl] = (stx[0] + stx[1]) + (stx[2] + stx[3])
-    for i in zs:
-        send(stz.at[zl], stz.at[zl], RQZ + zl, zdev(i))
-    slabs_sum(near)
+    stm[mate] = (stx[0] + stx[1]) + (stx[2] + stx[3])
+    for i in ms:
+        send(stm.at[mate], stm.at[mate], RQM + mate, mdev(i))
+    x_sum(far)
+    for i in ms:
+        arrived(stm.at[i], RQM + i)
+    stp[half] = (stm[0] + stm[1]) + (stm[2] + stm[3])
+    send(stp.at[half], stp.at[half], RQP, partner)
+    x_sum(near)
     bout[...] = mates_sum(far).astype(BF)
     send(bout, bin_, RB, partner)
     kept = shares_sum(zh)
-    g = mates_sum(near)
-
-    for i in zs:
-        arrived(stz.at[i], RQZ + i)
-    tot = stz[0]
-    for k in range(1, 8):
-        tot = tot + stz[k]
+    arrived(stp.at[1 - half], RQP)
+    tot = stp[0] + stp[1]
     gskip[...] = tot[:, 0:WID]
     ratio = resid[...] * jnp.exp(-2.0 * rt) / factor
     for m in range(MODES):
@@ -375,6 +407,7 @@
         carried = tot[:, WID * (5 + m) : WID * (6 + m)]
         gres[m : m + 1, :] = factor[m : m + 1, :] * paired
         grate[m : m + 1, :] = ratio[m : m + 1, :] * paired - carried
+    g = mates_sum(near)
 
     arrived(bin_, RB)
     gfin[d] = g + bin_[...].astype(F32)
@@ -443,8 +476,12 @@
             pltpu.VMEM((2, 4, SPAN, WID), BF),
             pltpu.VMEM((SPAN, WID), BF),
             pltpu.VMEM((SPAN, WID), BF),
-            pltpu.VMEM((2, 4, 4, 64, WID), BF),
-            pltpu.VMEM((2, 4, 4, 64, WID), BF),
+            pltpu.VMEM((2, 2, 2, 64, WID), BF),
+            pltpu.VMEM((2, 2, 2, 64, WID), BF),
+            pltpu.VMEM((2, 2, 2, 64, WID), F32),
+            pltpu.VMEM((2, 2, 2, 64, WID), BF),
+            pltpu.VMEM((2, 2, 2, 64, WID), BF),
+            pltpu.VMEM((2, 2, 2, 2, 64, WID), BF),
             pltpu.VMEM((2, 4, 64, WID), F32),
             pltpu.VMEM((2, 4, 64, WID), BF),
             pltpu.VMEM((2, 4, 64, WID), BF),
@@ -455,7 +492,8 @@
             pltpu.VMEM((8, WID, 2 * SPAN), BF),
             pltpu.VMEM((2, 1, NSTAT), F32),
             pltpu.VMEM((4, 1, NSTAT), F32),
-            pltpu.VMEM((8, 1, NSTAT), F32),
+            pltpu.VMEM((4, 1, NSTAT), F32),
+            pltpu.VMEM((2, 1, NSTAT), F32),
             pltpu.VMEM((MODES, WID), F32),
             pltpu.VMEM((MODES, WID), F32),
             pltpu.VMEM((1, WID), F32),

time: 82 us -> 79.7 us (0.972)
  Pallas kernels: 80.1 us -> 77.9 us
    pallas_call x1, Pallas kernels: 78.4 us -> 76.2 us  [body(): pl.pallas_call(kernel, out_shape=shapes, in_specs=[hbm] * 8, out_specs=(v...]
where the time goes in v3:
time: 79.7 us; the launch traced here: 78.6 us
  Pallas kernels  77.9 us (98%)
    pallas_call x1, Pallas kernels, body(): pl.pallas_call(kernel, out_shape=shapes, in_specs=[hbm] * 8, out_specs=(v...  76.2 us
    pallas_call x1, Pallas kernels, body(): pl.pallas_call(store, out_shape=shapes, in_specs=[vm] * 7, out_specs=(hbm...  1.71 us

profile of v3, /device:TPU:1, one launch (start us, length us, event | category | flops | bytes accessed | tf_op | source)
XLA Modules:
  0.0 78.6 jit_solution(9898998246888816688)
XLA Ops:
  0.6 76.2 %step.1 = (bf16[1,128,256]{2,1,0:T(8,128)(2,1)}, bf16[1,128,256]{2,1,0:T(8,128)(2,1)}, f32[64,256]{1,0:T(8,128)}, f32[64,256]{1,0:T(8,128)}, f32[1,256]{1,0:T(1,...) custom-call(bf16[1,128,256]{2,1,0:T(8,128)(2,1)} %tok.1, bf16[1,128,256]{2,1,0:T(8,128)(2,1)} %cot.1, bf16[64,256]{1,0:T(8,128)(2,1)} %wv.1, ...), custom_call_target="tpu_custom_call" | custom-call | tf_op jit(solution)/shard_map/step/pallas_call | solution.py:455
  76.9 1.7 %store.1 = (bf16[1,128,256]{2,1,0:T(8,128)(2,1)}, bf16[1,128,256]{2,1,0:T(8,128)(2,1)}, f32[64,256]{1,0:T(8,128)}, f32[64,256]{1,0:T(8,128)}, f32[1,256]{1,0:T(1...) custom-call(bf16[1,128,256]{2,1,0:T(8,128)(2,1)} %get-tuple-element.21.refs_0_, ...), custom_call_target="tpu_custom_call" | custom-call | tf_op jit(solution)/shard_map/store/pallas_call | solution.py:513

commit v4 on v3

--- a/solution.py
+++ b/solution.py
@@ -12,14 +12,16 @@
 WID = 256
 MODES = 4
 LINE = 8 * SPAN
-NSTAT = 9 * WID
+NSTAT = 9 * WID // 2
+PART = SPAN // 2
 
 RT, RZ, RX, RS, RF = 0, 16, 24, 32, 40
 RE, REX, RC, RP, RPA = 41, 49, 53, 54, 62
 RG, RR, RM, RB, RW2 = 63, 71, 75, 83, 84
-RQS, RQX, RQM, RQP = 85, 86, 90, 94
-NRECV = 95
-NSEND = 128
+RQS, RQX, RQM, RQP, RQ2 = 85, 86, 90, 94, 95
+RP2, RPA2 = 96, 104
+NRECV = 105
+NSEND = 140
 
 
 def dot(a, b, dims):
@@ -35,9 +37,9 @@
 def kernel(
     tok, cot, wv, wg, rate_h, resid_h, skip_h, clen_h,
     out, gtok, gwv, gwg, gskip, gres, grate,
-    fown, fsib, wb, cbuf, ep, em, sloc, bloc, sb, zb, xsb, xb,
+    fown, fsib, wb, cbuf, ep, em, sloc, bloc, sb, sh, zb, zf, xsb, xb,
     cb, cs, pout, pin, pa_out, pa_in, gr_out, gr_in, gk, gd, gc, gin, gown,
-    mout, min_, bout, bin_, gfin, wt, ft, stq, stx, stm, stp, rate, resid, skip, clen, ssem, rsem, lsem,
+    mout, min_, bout, bin_, gfin, wt, ft, stl, sti, stx, stm, stp, tfin, rate, resid, skip, clen, ssem, rsem, lsem,
 ):
     d = lax.axis_index("dp")
     c = lax.axis_index("ctx")
@@ -117,6 +119,8 @@
     factor = jnp.sqrt(one_minus_exp(2.0 * rt))
     wm = resid[...] * factor
     r1 = row(rt)
+    step_f = jnp.exp(-r1)
+    step_b = jnp.exp(-float(SPAN) * r1)
     tcol = lax.broadcasted_iota(jnp.int32, (SPAN, WID), 0).astype(F32)
     for m in range(MODES):
         rm = rt[m : m + 1, :]
@@ -205,16 +209,20 @@
     for i in (ms[1], ms[0], ms[2]):
         send(wb.at[d, x * 8 + k], wb.at[d, x * 8 + k], RZ + k, mdev(i))
     spread_x(k)
+    ta = (1 - zh) * 4 + y
+
+    def tokens_on(q):
+        arrived(piece(ta, q), RT + 2 * ta + q)
+        for i in ys:
+            send(piece(ta, q), piece(ta, q), RT + 2 * ta + q, ydev(i))
+
+    tokens_on(0)
     for i in ms:
         k = far * 4 + i
         arrived(wb.at[d, x * 8 + k], RZ + k)
         spread_x(k)
     to_sib(x, far)
-    ta = (1 - zh) * 4 + y
-    for q in range(2):
-        arrived(piece(ta, q), RT + 2 * ta + q)
-        for i in ys:
-            send(piece(ta, q), piece(ta, q), RT + 2 * ta + q, ydev(i))
+    tokens_on(1)
     for i in (xs[0], xs[2], xs[1]):
         arrived(quad(d, i, near), RX + 2 * i + near)
         to_sib(i, near)
@@ -252,9 +260,10 @@
         b = dot(upper, hi, mm) + dot(upper, lo, mm)
         bloc[m] = b
         sb[1:2, m * WID : (m + 1) * WID] = b[0:1, :]
-    zb[zl] = sb[...]
+    sh[...] = sb[...].astype(BF)
+    zb[zl] = sh[...]
     for i in (zs[6], zs[0], zs[5], zs[1], zs[4], zs[2], zs[3]):
-        send(sb, zb.at[zl], RE + zl, zdev(i))
+        send(sh, zb.at[zl], RE + zl, zdev(i))
     arrived(fsib, RF)
     for j in range(8):
         wt[j, 0:WID] = wblock(0, j).T
@@ -263,7 +272,9 @@
         ft[j, :, SPAN:] = fsib[j].T
     for i in zs:
         arrived(zb.at[i], RE + i)
-    fz, bz = zb[:, 0, :], zb[:, 1, :]
+    for i in range(8):
+        zf[i] = zb[i].astype(F32)
+    fz, bz = zf[:, 0, :], zf[:, 1, :]
     xsb[0:1, :] = jnp.sum(w_tot_f * fz, axis=0, keepdims=True)
     xsb[1:2, :] = jnp.sum(w_tot_b * bz, axis=0, keepdims=True)
     xb[x] = xsb[...]
@@ -275,48 +286,76 @@
         arrived(xb.at[i], REX + i)
     inc_f = inc_f + jnp.sum(w_x_f * xb[:, 0, :], axis=0, keepdims=True)
     inc_b = inc_b + jnp.sum(w_x_b * xb[:, 1, :], axis=0, keepdims=True)
-    inc_f = inc_f * jnp.exp(-r1)
-    inc_b = inc_b * jnp.exp(-float(SPAN) * r1)
+    inc_f = inc_f * step_f
+    inc_b = inc_b * step_b
 
     sk = skip[...]
     mixed = sk * value
     gval = sk * gm
-    stq[d, :, 0:WID] = jnp.sum(gm * value, axis=0, keepdims=True)
+    pairs, carries = [], []
     for m in range(MODES):
         lanes = slice(m * WID, (m + 1) * WID)
         state = em[m] * (sloc[m] + clearf * inc_f[:, lanes])
         gst = ep[m] * (bloc[m] + clearb * inc_b[:, lanes])
         mixed = mixed + wm[m : m + 1, :] * state
         gval = gval + gst
-        lo = WID * (1 + m)
-        stq[d, :, lo : lo + WID] = jnp.sum(gm * state, axis=0, keepdims=True)
-        lo = WID * (5 + m)
-        stq[d, :, lo : lo + WID] = jnp.sum(gst * (state - value), axis=0, keepdims=True)
+        pairs.append(jnp.sum(gm * state, axis=0, keepdims=True))
+        carries.append(jnp.sum(gst * (state - value), axis=0, keepdims=True))
+    stats = [jnp.sum(gm * value, axis=0, keepdims=True)] + pairs + carries
+    stats = jnp.concatenate(stats, axis=1)
+    stl[0] = stats[:, 0:NSTAT]
+    stl[1] = stats[:, NSTAT:]
     out[0] = (gate * mixed).astype(BF)
     cv = gval.astype(BF)
     cg = (upstream * mixed).astype(BF)
     cb[0] = cv
     cb[1] = cg
     send(cb.at[1 - d], cs, RC, sib)
-    send(stq.at[d], stq.at[d], RQS, sib)
+    send(stl.at[1 - d], sti, RQS, sib)
 
     both = jnp.concatenate([cv, cg], axis=1)
 
     def share(h, i):
         return dot(both, wt[h * 4 + i], mm).astype(BF)
 
-    def shares(h):
+    def rows(p):
+        return slice(p * PART, (p + 1) * PART)
+
+    def other_shares(p, sem):
+        h = 1 - zh
+        for i in (ys[1], ys[0], ys[2], y):
+            part = dot(both[rows(p)], wt[h * 4 + i], mm).astype(BF)
+            if i is y:
+                pin[h, y, rows(p)] = part
+                continue
+            pout[h, i, rows(p)] = part
+            src = pout.at[h, i, pl.ds(p * PART, PART)]
+            dst = pin.at[h, y, pl.ds(p * PART, PART)]
+            send(src, dst, sem + 4 * h + y, ydev(i))
+
+    def other_sum(p, sem):
+        h = 1 - zh
+        for i in ys:
+            arrived(pin.at[h, i, pl.ds(p * PART, PART)], sem + 4 * h + i)
+        total = pin[h, 0, rows(p)].astype(F32)
+        for k in range(1, 4):
+            total = total + pin[h, k, rows(p)].astype(F32)
+        pa_out[rows(p)] = total.astype(BF)
+        cut = pl.ds(p * PART, PART)
+        send(pa_out.at[cut], pa_in.at[cut], RPA if p == 0 else RPA2, anti)
+
+    def own_shares():
         for i in (ys[1], ys[0], ys[2]):
-            pout[h, i] = share(h, i)
-            send(pout.at[h, i], pin.at[h, y], RP + 4 * h + y, ydev(i))
-        pin[h, y] = share(h, y)
-
-    def shares_sum(h):
+            pout[zh, i] = share(zh, i)
+            send(pout.at[zh, i], pin.at[zh, y], RP + 4 * zh + y, ydev(i))
+        pin[zh, y] = share(zh, y)
+
+    def own_sum():
         for i in ys:
-            arrived(pin.at[h, i], RP + 4 * h + i)
-        total = pin[h, 0].astype(F32)
+            arrived(pin.at[zh, i], RP + 4 * zh + i)
+        total = pin[zh, 0].astype(F32)
         for k in range(1, 4):
-            total = total + pin[h, k].astype(F32)
+            total = total + pin[zh, k].astype(F32)
         return total
 
     right, left = xs[0], xs[2]
@@ -366,40 +405,49 @@
             g = g + min_[h, i].astype(F32)
         return g
 
-    shares(1 - zh)
-    arrived(stq.at[1 - d], RQS)
-    stx[x] = stq[0] + stq[1]
+    other_shares(0, RP)
+    arrived(sti, RQS)
+    stx[x] = stl[d] + sti[...]
     for i in xs:
         send(stx.at[x], stx.at[x], RQX + x, xdev(i))
     arrived(cs, RC)
     cots = jnp.concatenate([cb[d], cs[...]], axis=0)
     x_start(far)
+    other_shares(1, RP2)
     x_direct(far)
     x_start(near)
-    shares(zh)
+    own_shares()
+    other_sum(0, RP)
+    x_relay(far)
+    x_direct(near)
+    other_sum(1, RP2)
     for h in (far, near):
         gown[h] = slab(h, x)
-    x_relay(far)
-    x_direct(near)
-    pa_out[...] = shares_sum(1 - zh).astype(BF)
-    send(pa_out, pa_in, RPA, anti)
-    x_relay(near)
     for i in xs:
         arrived(stx.at[i], RQX + i)
     stm[mate] = (stx[0] + stx[1]) + (stx[2] + stx[3])
     for i in ms:
         send(stm.at[mate], stm.at[mate], RQM + mate, mdev(i))
+    x_relay(near)
     x_sum(far)
+    x_sum(near)
     for i in ms:
         arrived(stm.at[i], RQM + i)
     stp[half] = (stm[0] + stm[1]) + (stm[2] + stm[3])
-    send(stp.at[half], stp.at[half], RQP, partner)
-    x_sum(near)
     bout[...] = mates_sum(far).astype(BF)
     send(bout, bin_, RB, partner)
-    kept = shares_sum(zh)
+    send(stp.at[half], stp.at[half], RQP, partner)
+    kept = own_sum()
+    g = mates_sum(near)
     arrived(stp.at[1 - half], RQP)
-    tot = stp[0] + stp[1]
+    tfin[d] = stp[0] + stp[1]
+    send(tfin.at[d], tfin.at[d], RQ2, sib)
+
+    arrived(bin_, RB)
+    gfin[d] = g + bin_[...].astype(F32)
+    send(gfin.at[d], gfin.at[d], RW2, sib)
+    arrived(tfin.at[1 - d], RQ2)
+    tot = jnp.concatenate([tfin[0], tfin[1]], axis=1)
     gskip[...] = tot[:, 0:WID]
     ratio = resid[...] * jnp.exp(-2.0 * rt) / factor
     for m in range(MODES):
@@ -407,12 +455,8 @@
         carried = tot[:, WID * (5 + m) : WID * (6 + m)]
         gres[m : m + 1, :] = factor[m : m + 1, :] * paired
         grate[m : m + 1, :] = ratio[m : m + 1, :] * paired - carried
-    g = mates_sum(near)
-
-    arrived(bin_, RB)
-    gfin[d] = g + bin_[...].astype(F32)
-    send(gfin.at[d], gfin.at[d], RW2, sib)
-    arrived(pa_in, RPA)
+    for p, sem in ((0, RPA), (1, RPA2)):
+        arrived(pa_in.at[pl.ds(p * PART, PART)], sem)
     gtok[0] = (kept + pa_in[...].astype(F32)).astype(BF)
     arrived(gfin.at[1 - d], RW2)
     gwv[...] = gfin[0]
@@ -467,6 +511,8 @@
             pltpu.VMEM((MODES, SPAN, WID), F32),
             pltpu.VMEM((MODES, SPAN, WID), F32),
             pltpu.VMEM((2, MODES * WID), F32),
+            pltpu.VMEM((2, MODES * WID), BF),
+            pltpu.VMEM((8, 2, MODES * WID), BF),
             pltpu.VMEM((8, 2, MODES * WID), F32),
             pltpu.VMEM((2, MODES * WID), F32),
             pltpu.VMEM((4, 2, MODES * WID), F32),
@@ -491,8 +537,10 @@
             pltpu.VMEM((8, 2 * WID, WID), BF),
             pltpu.VMEM((8, WID, 2 * SPAN), BF),
             pltpu.VMEM((2, 1, NSTAT), F32),
+            pltpu.VMEM((1, NSTAT), F32),
             pltpu.VMEM((4, 1, NSTAT), F32),
             pltpu.VMEM((4, 1, NSTAT), F32),
+            pltpu.VMEM((2, 1, NSTAT), F32),
             pltpu.VMEM((2, 1, NSTAT), F32),
             pltpu.VMEM((MODES, WID), F32),
             pltpu.VMEM((MODES, WID), F32),

time: 79.7 us -> 77.2 us (0.969); the launches traced: 78.6 us -> 77 us
  Pallas kernels: 77.9 us -> 76.3 us
    pallas_call x1, Pallas kernels: 76.2 us -> 74.6 us  [body(): pl.pallas_call(kernel, out_shape=shapes, in_specs=[hbm] * 8, out_specs=(v...]
where the time goes in v4:
time: 77.2 us; the launch traced here: 77 us
  Pallas kernels  76.3 us (99%)
    pallas_call x1, Pallas kernels, body(): pl.pallas_call(kernel, out_shape=shapes, in_specs=[hbm] * 8, out_specs=(v...  74.6 us
    pallas_call x1, Pallas kernels, body(): pl.pallas_call(store, out_shape=shapes, in_specs=[vm] * 7, out_specs=(hbm...  1.71 us

profile of v4, /device:TPU:1, one launch (start us, length us, event | category | flops | bytes accessed | tf_op | source)
XLA Modules:
  0.0 77.0 jit_solution(6608744865545124501)
XLA Ops:
  0.6 74.6 %step.1 = (bf16[1,128,256]{2,1,0:T(8,128)(2,1)}, bf16[1,128,256]{2,1,0:T(8,128)(2,1)}, f32[64,256]{1,0:T(8,128)}, f32[64,256]{1,0:T(8,128)}, f32[1,256]{1,0:T(1,...) custom-call(bf16[1,128,256]{2,1,0:T(8,128)(2,1)} %tok.1, bf16[1,128,256]{2,1,0:T(8,128)(2,1)} %cot.1, bf16[64,256]{1,0:T(8,128)(2,1)} %wv.1, ...), custom_call_target="tpu_custom_call" | custom-call | tf_op jit(solution)/shard_map/step/pallas_call | solution.py:499
  75.3 1.7 %store.1 = (bf16[1,128,256]{2,1,0:T(8,128)(2,1)}, bf16[1,128,256]{2,1,0:T(8,128)(2,1)}, f32[64,256]{1,0:T(8,128)}, f32[64,256]{1,0:T(8,128)}, f32[1,256]{1,0:T(1...) custom-call(bf16[1,128,256]{2,1,0:T(8,128)(2,1)} %get-tuple-element.21.refs_0_, ...), custom_call_target="tpu_custom_call" | custom-call | tf_op jit(solution)/shard_map/store/pallas_call | solution.py:561

commit v5 on v4

--- a/solution.py
+++ b/solution.py
@@ -37,7 +37,7 @@
 def kernel(
     tok, cot, wv, wg, rate_h, resid_h, skip_h, clen_h,
     out, gtok, gwv, gwg, gskip, gres, grate,
-    fown, fsib, wb, cbuf, ep, em, sloc, bloc, sb, sh, zb, zf, xsb, xb,
+    fown, fsib, wb, cbuf, ep, em, sloc, bloc, sb, sh, zb, wtot, win, wx, xsb, xb,
     cb, cs, pout, pin, pa_out, pa_in, gr_out, gr_in, gk, gd, gc, gin, gown,
     mout, min_, bout, bin_, gfin, wt, ft, stl, sti, stx, stm, stp, tfin, rate, resid, skip, clen, ssem, rsem, lsem,
 ):
@@ -119,8 +119,6 @@
     factor = jnp.sqrt(one_minus_exp(2.0 * rt))
     wm = resid[...] * factor
     r1 = row(rt)
-    step_f = jnp.exp(-r1)
-    step_b = jnp.exp(-float(SPAN) * r1)
     tcol = lax.broadcasted_iota(jnp.int32, (SPAN, WID), 0).astype(F32)
     for m in range(MODES):
         rm = rt[m : m + 1, :]
@@ -136,24 +134,27 @@
     clearf = jnp.where(stc == seg_prev, 1.0, 0.0)
     clearb = jnp.where(stc == seg_next, 1.0, 0.0)
 
-    k8 = lax.broadcasted_iota(jnp.int32, (8, MODES * WID), 0)
-    k4 = lax.broadcasted_iota(jnp.int32, (4, MODES * WID), 0)
-
-    def weight(ok, dist):
-        return jnp.where(ok, jnp.exp(-r1 * jnp.maximum(dist, 0).astype(F32)), 0.0)
-
+    back = lax.broadcasted_iota(jnp.int32, (2, MODES * WID), 0) == 1
     base = x * LINE
-    endpos = base + SPAN * k8 + (SPAN - 1)
-    topos = base + SPAN * k8
-    seg_end, seg_top = seg(endpos), seg(topos)
-    w_tot_f = weight(seg_end == seg(base + LINE - 1), base + LINE - 1 - endpos)
-    w_tot_b = weight(seg_top == seg(base), topos - base)
-    w_in_f = weight((k8 < zl) & (seg_end == seg_prev), first - 1 - endpos)
-    w_in_b = weight((k8 > zl) & (seg_top == seg_next), topos - (first + SPAN))
-    xend = (k4 + 1) * LINE - 1
-    xtop = k4 * LINE
-    w_x_f = weight((k4 < x) & (seg(xend) == seg_prev), first - 1 - xend)
-    w_x_b = weight((k4 > x) & (seg(xtop) == seg_next), xtop - (first + SPAN))
+
+    def weight(source, target, later_ok, earlier_ok):
+        dist = jnp.where(back, source[1] - target[1], target[0] - source[0])
+        ok_f = earlier_ok & (seg(source[0]) == seg(target[0]))
+        ok_b = later_ok & (seg(source[1]) == seg(target[1]))
+        scale = jnp.exp(-r1 * jnp.maximum(dist, 0).astype(F32))
+        keep = jnp.where(back, ok_b.astype(F32), ok_f.astype(F32))
+        return scale * keep
+
+    yes = c >= 0
+    here = (first - 1, first + SPAN)
+    for k in range(8):
+        ends = (base + SPAN * k + SPAN - 1, base + SPAN * k)
+        wtot[k] = weight(ends, (base + LINE - 1, base), yes, yes)
+        win[k] = weight(ends, here, k > zl, k < zl)
+    for k in range(4):
+        ends = ((k + 1) * LINE - 1, k * LINE)
+        wx[k] = weight(ends, here, k > x, k < x)
+    step2 = jnp.exp(-r1 * jnp.where(back, float(SPAN), 1.0))
 
     sends = []
 
@@ -272,22 +273,22 @@
         ft[j, :, SPAN:] = fsib[j].T
     for i in zs:
         arrived(zb.at[i], RE + i)
-    for i in range(8):
-        zf[i] = zb[i].astype(F32)
-    fz, bz = zf[:, 0, :], zf[:, 1, :]
-    xsb[0:1, :] = jnp.sum(w_tot_f * fz, axis=0, keepdims=True)
-    xsb[1:2, :] = jnp.sum(w_tot_b * bz, axis=0, keepdims=True)
-    xb[x] = xsb[...]
-    for i in xs:
+    total = wtot[0] * zb[0].astype(F32)
+    for k in range(1, 8):
+        total = total + wtot[k] * zb[k].astype(F32)
+    xsb[...] = total
+    xb[x] = total
+    for i in (xs[1], xs[0], xs[2]):
         send(xsb, xb.at[x], REX + x, xdev(i))
-    inc_f = jnp.sum(w_in_f * fz, axis=0, keepdims=True)
-    inc_b = jnp.sum(w_in_b * bz, axis=0, keepdims=True)
+    inc = win[0] * zb[0].astype(F32)
+    for k in range(1, 8):
+        inc = inc + win[k] * zb[k].astype(F32)
     for i in xs:
         arrived(xb.at[i], REX + i)
-    inc_f = inc_f + jnp.sum(w_x_f * xb[:, 0, :], axis=0, keepdims=True)
-    inc_b = inc_b + jnp.sum(w_x_b * xb[:, 1, :], axis=0, keepdims=True)
-    inc_f = inc_f * step_f
-    inc_b = inc_b * step_b
+    for k in range(4):
+        inc = inc + wx[k] * xb[k]
+    inc = inc * step2
+    inc_f, inc_b = inc[0:1, :], inc[1:2, :]
 
     sk = skip[...]
     mixed = sk * value
@@ -434,9 +435,9 @@
     for i in ms:
         arrived(stm.at[i], RQM + i)
     stp[half] = (stm[0] + stm[1]) + (stm[2] + stm[3])
+    send(stp.at[half], stp.at[half], RQP, partner)
     bout[...] = mates_sum(far).astype(BF)
     send(bout, bin_, RB, partner)
-    send(stp.at[half], stp.at[half], RQP, partner)
     kept = own_sum()
     g = mates_sum(near)
     arrived(stp.at[1 - half], RQP)
@@ -514,6 +515,8 @@
             pltpu.VMEM((2, MODES * WID), BF),
             pltpu.VMEM((8, 2, MODES * WID), BF),
             pltpu.VMEM((8, 2, MODES * WID), F32),
+            pltpu.VMEM((8, 2, MODES * WID), F32),
+            pltpu.VMEM((4, 2, MODES * WID), F32),
             pltpu.VMEM((2, MODES * WID), F32),
             pltpu.VMEM((4, 2, MODES * WID), F32),
             pltpu.VMEM((2, SPAN, WID), BF),

time: 77.2 us -> 77 us (level)
  no operation moved by 1% of the time
where the time goes in v5:
time: 77 us; the launch traced here: 76.8 us
  Pallas kernels  76.1 us (99%)
    pallas_call x1, Pallas kernels, body(): pl.pallas_call(kernel, out_shape=shapes, in_specs=[hbm] * 8, out_specs=(v...  74.4 us
    pallas_call x1, Pallas kernels, body(): pl.pallas_call(store, out_shape=shapes, in_specs=[vm] * 7, out_specs=(hbm...  1.71 us

profile of v5, /device:TPU:1, one launch (start us, length us, event | category | flops | bytes accessed | tf_op | source)
XLA Modules:
  0.0 76.8 jit_solution(11230859686214595578)
XLA Ops:
  0.6 74.4 %step.1 = (bf16[1,128,256]{2,1,0:T(8,128)(2,1)}, bf16[1,128,256]{2,1,0:T(8,128)(2,1)}, f32[64,256]{1,0:T(8,128)}, f32[64,256]{1,0:T(8,128)}, f32[1,256]{1,0:T(1,...) custom-call(bf16[1,128,256]{2,1,0:T(8,128)(2,1)} %tok.1, bf16[1,128,256]{2,1,0:T(8,128)(2,1)} %cot.1, bf16[64,256]{1,0:T(8,128)(2,1)} %wv.1, ...), custom_call_target="tpu_custom_call" | custom-call | tf_op jit(solution)/shard_map/step/pallas_call | solution.py:500
  75.1 1.7 %store.1 = (bf16[1,128,256]{2,1,0:T(8,128)(2,1)}, bf16[1,128,256]{2,1,0:T(8,128)(2,1)}, f32[64,256]{1,0:T(8,128)}, f32[64,256]{1,0:T(8,128)}, f32[1,256]{1,0:T(1...) custom-call(bf16[1,128,256]{2,1,0:T(8,128)(2,1)} %get-tuple-element.21.refs_0_, ...), custom_call_target="tpu_custom_call" | custom-call | tf_op jit(solution)/shard_map/store/pallas_call | solution.py:564

commit v6 on v5

--- a/solution.py
+++ b/solution.py
@@ -20,8 +20,9 @@
 RG, RR, RM, RB, RW2 = 63, 71, 75, 83, 84
 RQS, RQX, RQM, RQP, RQ2 = 85, 86, 90, 94, 95
 RP2, RPA2 = 96, 104
-NRECV = 105
-NSEND = 140
+RM2, RB2 = 105, 109
+NRECV = 110
+NSEND = 144
 
 
 def dot(a, b, dims):
@@ -395,16 +396,33 @@
             g = gown[h, 2 * part : 2 * part + 2]
             g = g + gin[h, 0, part].astype(F32) + gin[h, 1, part].astype(F32)
             mout[h, 2 * part : 2 * part + 2] = g.astype(BF)
-        for i in (ms[1], ms[0], ms[2]):
-            send(mout.at[h, i], min_.at[h, mate], RM + 4 * h + mate, mdev(i))
-
-    def mates_sum(h):
+        if h is near:
+            for i in (ms[1], ms[0], ms[2]):
+                send(mout.at[h, i], min_.at[h, mate], RM + 4 * h + mate, mdev(i))
+            return
+        for r, sem in ((0, RM + 4 * h), (1, RM2)):
+            for i in (ms[1], ms[0], ms[2]):
+                cut = pl.ds(32 * r, 32)
+                send(mout.at[h, i, cut], min_.at[h, mate, cut], sem + mate, mdev(i))
+
+    def mates_near():
         for i in ms:
-            arrived(min_.at[h, i], RM + 4 * h + i)
-        g = mout[h, mate].astype(F32)
+            arrived(min_.at[near, i], RM + 4 * near + i)
+        g = mout[near, mate].astype(F32)
         for i in ms:
-            g = g + min_[h, i].astype(F32)
+            g = g + min_[near, i].astype(F32)
         return g
+
+    def mates_far(r, sem, out_sem):
+        cut = slice(32 * r, 32 * r + 32)
+        part = pl.ds(32 * r, 32)
+        for i in ms:
+            arrived(min_.at[far, i, part], sem + i)
+        g = mout[far, mate, cut].astype(F32)
+        for i in ms:
+            g = g + min_[far, i, cut].astype(F32)
+        bout[cut] = g.astype(BF)
+        send(bout.at[part], bin_.at[part], out_sem, partner)
 
     other_shares(0, RP)
     arrived(sti, RQS)
@@ -436,15 +454,16 @@
         arrived(stm.at[i], RQM + i)
     stp[half] = (stm[0] + stm[1]) + (stm[2] + stm[3])
     send(stp.at[half], stp.at[half], RQP, partner)
-    bout[...] = mates_sum(far).astype(BF)
-    send(bout, bin_, RB, partner)
+    mates_far(0, RM + 4 * far, RB)
+    mates_far(1, RM2, RB2)
     kept = own_sum()
-    g = mates_sum(near)
+    g = mates_near()
     arrived(stp.at[1 - half], RQP)
     tfin[d] = stp[0] + stp[1]
     send(tfin.at[d], tfin.at[d], RQ2, sib)
 
-    arrived(bin_, RB)
+    arrived(bin_.at[pl.ds(0, 32)], RB)
+    arrived(bin_.at[pl.ds(32, 32)], RB2)
     gfin[d] = g + bin_[...].astype(F32)
     send(gfin.at[d], gfin.at[d], RW2, sib)
     arrived(tfin.at[1 - d], RQ2)
@@ -462,6 +481,7 @@
     arrived(gfin.at[1 - d], RW2)
     gwv[...] = gfin[0]
     gwg[...] = gfin[1]
+    assert len(sends) <= NSEND
     for cp in sends:
         cp.wait_send()
 
@@ -554,12 +574,17 @@
             pltpu.SemaphoreType.DMA((7,)),
         ],
         compiler_params=pltpu.CompilerParams(
-            collective_id=0, has_side_effects=True, vmem_limit_bytes=67043328
+            collective_id=0, has_side_effects=True, vmem_limit_bytes=48 << 20
         ),
         name="step",
     )(
-        tokens, cotangent, w_value, w_gate, decay_rate, residue,
-        skip_gain.reshape(1, WID), contig_len,
+        *[
+            pltpu.with_memory_space_constraint(a, pltpu.HBM)
+            for a in (
+                tokens, cotangent, w_value, w_gate, decay_rate, residue,
+                skip_gain.reshape(1, WID), contig_len,
+            )
+        ]
     )
     outs = pl.pallas_call(
         store,
@@ -567,6 +592,7 @@
         in_specs=[vm] * 7,
         out_specs=(hbm,) * 7,
         scratch_shapes=[pltpu.SemaphoreType.DMA((7,))],
+        compiler_params=pltpu.CompilerParams(vmem_limit_bytes=1 << 20),
         name="store",
     )(*outs)
     outs = list(outs)

time: 77 us -> 76.6 us (level)
    pallas_call x1, Pallas kernels: 1.71 us -> 0.76 us  [body(): pl.pallas_call(store, out_shape=shapes, in_specs=[vm] * 7, out_specs=(hbm...]
where the time goes in v6:
time: 76.6 us; the launch traced here: 76.5 us
  Pallas kernels  75.8 us (99%)
    pallas_call x1, Pallas kernels, body(): pl.pallas_call(kernel, out_shape=shapes, in_specs=[hbm] * 8, out_specs=(v...  75.1 us

profile of v6, /device:TPU:1, one launch (start us, length us, event | category | flops | bytes accessed | tf_op | source)
XLA Modules:
  0.0 76.5 jit_solution(3562487538894101017)
XLA Ops:
  0.6 75.1 %step.1 = (bf16[1,128,256]{2,1,0:T(8,128)(2,1)S(1)}, bf16[1,128,256]{2,1,0:T(8,128)(2,1)S(1)}, f32[64,256]{1,0:T(8,128)S(1)}, f32[64,256]{1,0:T(8,128)S(1)}, f32...) custom-call(bf16[1,128,256]{2,1,0:T(8,128)(2,1)} %tok.1, bf16[1,128,256]{2,1,0:T(8,128)(2,1)} %cot.1, ...), custom_call_target="tpu_custom_call" | custom-call | tf_op jit(solution)/shard_map/step/pallas_call | solution.py:520
  75.7 0.8 %store.1 = (bf16[1,128,256]{2,1,0:T(8,128)(2,1)}, bf16[1,128,256]{2,1,0:T(8,128)(2,1)}, f32[64,256]{1,0:T(8,128)}, f32[64,256]{1,0:T(8,128)}, f32[1,256]{1,0:T(1...) custom-call(bf16[1,128,256]{2,1,0:T(8,128)(2,1)S(1)} %get-tuple-element.21.refs_0_, ...), custom_call_target="tpu_custom_call" | custom-call | tf_op jit(solution)/shard_map/store/pallas_call | solution.py:589

commit v7 on v6

--- a/solution.py
+++ b/solution.py
@@ -69,6 +69,16 @@
     def mdev(k):
         return {"ctx": x * 8 + half * 4 + k}
 
+    barrier = pltpu.get_barrier_semaphore()
+    peers = (
+        [sib, anti]
+        + [ydev(k) for k in ys]
+        + [xdev(k) for k in xs]
+        + [zdev(k) for k in zs]
+    )
+    for who in peers:
+        pl.semaphore_signal(barrier, inc=1, device_id=who, device_id_type=MESH)
+
     loads = [
         pltpu.make_async_copy(tok.at[0], fown.at[t], lsem.at[0]),
         pltpu.make_async_copy(cot.at[0], cbuf, lsem.at[1]),
@@ -89,16 +99,6 @@
     @pl.when(d == 1)
     def _():
         pltpu.make_async_copy(wg, wb.at[1, c], lsem.at[2]).start()
-
-    barrier = pltpu.get_barrier_semaphore()
-    peers = (
-        [sib, anti]
-        + [ydev(k) for k in ys]
-        + [xdev(k) for k in xs]
-        + [zdev(k) for k in zs]
-    )
-    for who in peers:
-        pl.semaphore_signal(barrier, inc=1, device_id=who, device_id_type=MESH)
 
     for cp in small:
         cp.wait()

time: 76.6 us -> 76.8 us (level)
  no operation moved by 1% of the time
where the time goes in v7:
time: 76.8 us; the launch traced here: 76.6 us
  Pallas kernels  76 us (99%)
    pallas_call x1, Pallas kernels, body(): pl.pallas_call(kernel, out_shape=shapes, in_specs=[hbm] * 8, out_specs=(v...  75.2 us

profile of v7, /device:TPU:1, one launch (start us, length us, event | category | flops | bytes accessed | tf_op | source)
XLA Modules:
  0.0 76.6 jit_solution(15061639517546978820)
XLA Ops:
  0.6 75.2 %step.1 = (bf16[1,128,256]{2,1,0:T(8,128)(2,1)S(1)}, bf16[1,128,256]{2,1,0:T(8,128)(2,1)S(1)}, f32[64,256]{1,0:T(8,128)S(1)}, f32[64,256]{1,0:T(8,128)S(1)}, f32...) custom-call(bf16[1,128,256]{2,1,0:T(8,128)(2,1)} %tok.1, bf16[1,128,256]{2,1,0:T(8,128)(2,1)} %cot.1, ...), custom_call_target="tpu_custom_call" | custom-call | tf_op jit(solution)/shard_map/step/pallas_call | solution.py:520
  75.9 0.8 store.1

commit v8 on v7

--- a/solution.py
+++ b/solution.py
@@ -435,11 +435,11 @@
     other_shares(1, RP2)
     x_direct(far)
     x_start(near)
-    own_shares()
     other_sum(0, RP)
     x_relay(far)
     x_direct(near)
     other_sum(1, RP2)
+    own_shares()
     for h in (far, near):
         gown[h] = slab(h, x)
     for i in xs:

time: 76.8 us -> 75.2 us (0.979)
  Pallas kernels: 76 us -> 74.4 us
    pallas_call x1, Pallas kernels: 75.2 us -> 73.6 us  [body(): pl.pallas_call(kernel, out_shape=shapes, in_specs=[hbm] * 8, out_specs=(v...]
where the time goes in v8:
time: 75.2 us; the launch traced here: 75 us
  Pallas kernels  74.4 us (99%)
    pallas_call x1, Pallas kernels, body(): pl.pallas_call(kernel, out_shape=shapes, in_specs=[hbm] * 8, out_specs=(v...  73.6 us

profile of v8, /device:TPU:1, one launch (start us, length us, event | category | flops | bytes accessed | tf_op | source)
XLA Modules:
  0.0 75.0 jit_solution(10614186134148264690)
XLA Ops:
  0.6 73.6 %step.1 = (bf16[1,128,256]{2,1,0:T(8,128)(2,1)S(1)}, bf16[1,128,256]{2,1,0:T(8,128)(2,1)S(1)}, f32[64,256]{1,0:T(8,128)S(1)}, f32[64,256]{1,0:T(8,128)S(1)}, f32...) custom-call(bf16[1,128,256]{2,1,0:T(8,128)(2,1)} %tok.1, bf16[1,128,256]{2,1,0:T(8,128)(2,1)} %cot.1, ...), custom_call_target="tpu_custom_call" | custom-call | tf_op jit(solution)/shard_map/step/pallas_call | solution.py:520
  74.3 0.8 %store.1 = (bf16[1,128,256]{2,1,0:T(8,128)(2,1)}, bf16[1,128,256]{2,1,0:T(8,128)(2,1)}, f32[64,256]{1,0:T(8,128)}, f32[64,256]{1,0:T(8,128)}, f32[1,256]{1,0:T(1...) custom-call(bf16[1,128,256]{2,1,0:T(8,128)(2,1)S(1)} %get-tuple-element.21.refs_0_, ...), custom_call_target="tpu_custom_call" | custom-call | tf_op jit(solution)/shard_map/store/pallas_call | solution.py:589
